TPU v7x, 32 devices: a whole 2x2x4 slice. The times are simulated.
32 devices in a mesh: dp: 16 (over z, x, core), mp: 2 (over y).
Axes of the slice: x: 2, y: 2, z: 4, core: 2. Of those that a mesh axis runs over, the one named last changes fastest.
Arguments:
- tokens: bfloat16 [64, 512, 768], P('dp', 'mp'), may hold values from -6 to 6
- lengths: int32 [64], P('dp'), may hold values from 128 to 512, as said below
- out_grad: bfloat16 [64, 512, 768], P('dp', 'mp'), may hold values from -6 to 6
- ln1_gain: float32 [768], replicated, may hold values from 0.25 to 1.75
- ln1_shift: float32 [768], replicated, may hold values from -1.75 to 1.75
- w_query: bfloat16 [768, 768], P(None, 'mp'), may hold values from -0.21875 to 0.21875
- b_query: float32 [768], P('mp'), may hold values from -3 to 3
- w_key: bfloat16 [768, 768], P(None, 'mp'), may hold values from -0.21875 to 0.21875
- w_value: bfloat16 [768, 768], P(None, 'mp'), may hold values from -0.21875 to 0.21875
- b_value: float32 [768], P('mp'), may hold values from -3 to 3
- w_out: bfloat16 [768, 768], P('mp'), may hold values from -1.75 to 1.75
- b_out: float32 [768], replicated, may hold values from -1.75 to 1.75
- ln2_gain: float32 [768], replicated, may hold values from 0.25 to 1.75
- ln2_shift: float32 [768], replicated, may hold values from -1.75 to 1.75
- w_up: bfloat16 [768, 3072], P(None, 'mp'), may hold values from -0.21875 to 0.21875
- b_up: float32 [3072], P('mp'), may hold values from -3 to 3
- w_down: bfloat16 [3072, 768], P('mp'), may hold values from -0.109375 to 0.109375
- b_down: float32 [768], replicated, may hold values from -1.75 to 1.75
Outputs:
- block_out: bfloat16 [64, 512, 768], P('dp', 'mp')
- input_grad: float32 [64, 512, 768], P('dp', 'mp')
- grad_ln1_gain: float32 [768], replicated
- grad_ln1_shift: float32 [768], replicated
- grad_w_query: float32 [768, 768], P(None, 'mp')
- grad_b_query: float32 [768], P('mp')
- grad_w_key: float32 [768, 768], P(None, 'mp')
- grad_w_value: float32 [768, 768], P(None, 'mp')
- grad_b_value: float32 [768], P('mp')
- grad_w_out: float32 [768, 768], P('mp')
- grad_b_out: float32 [768], replicated
- grad_ln2_gain: float32 [768], replicated
- grad_ln2_shift: float32 [768], replicated
- grad_w_up: float32 [768, 3072], P(None, 'mp')
- grad_b_up: float32 [3072], P('mp')
- grad_w_down: float32 [3072, 768], P('mp')
- grad_b_down: float32 [768], replicated
Inputs may be any that keep to these rules, and one draw needn't show every extreme that they name: lengths of the rows; some row has 512 and some row a quarter of 512.
All inputs are finite; a program needn't handle non-finite values.
Results may differ from a plain program's by a relative error of at most 0.013.
The roundings to bfloat16 on the way count: a program that leaves them out, or rounds other values in their place, can miss the bound.
Values may be sent and summed in bfloat16 or wider, within the bound.
No kernel may reach another device: no remote copies, remote signals or barrier semaphores. Data moves between devices by JAX's collectives and lax.ppermute only.
A program may use at most 192 MiB of HBM per device.

v0:
```python
import math

import jax
import jax.numpy as jnp
from jax import lax
from jax.sharding import PartitionSpec as P

HEAD_DIM = 64
SEQ = 512
MB = 4
ROWS_MB = 1


epsilon = 1e-12
masked_fill = -1000000000.0


def layer_norm(values, gain_vec, offset):
    average = jnp.mean(values, axis=-1, keepdims=True)
    centred = values - average
    inv_std = lax.rsqrt(jnp.mean(centred * centred, axis=-1, keepdims=True) + epsilon)
    unit_part = centred * inv_std
    return (unit_part * gain_vec + offset, unit_part, inv_std)


def norm_back(upstream, unit_part, inv_std, gain_vec):
    scaled = upstream * gain_vec
    return inv_std * (
        scaled
        - jnp.mean(scaled, axis=-1, keepdims=True)
        - unit_part * jnp.mean(scaled * unit_part, axis=-1, keepdims=True)
    )


def gelu_slope(values):
    normal_cdf = 0.5 * (1.0 + lax.erf(values * (1.0 / math.sqrt(2.0))))
    return normal_cdf + values * jnp.exp(-0.5 * values * values) * (1.0 / math.sqrt(2.0 * math.pi))


def product(pattern, left_side, right_side):
    return jnp.einsum(pattern, left_side, right_side, preferred_element_type=jnp.float32)


def token_sum(values):
    return jnp.sum(values, axis=(0, 1))


def masked_scores(query_low, keys_low, key_valid, score_scale):
    raw_scores = product("bqhd,bkhd->bhqk", query_low, keys_low) * score_scale
    return jnp.where(key_valid, raw_scores, masked_fill)


def on_device(
    tokens,
    lengths,
    out_grad,
    ln1_gain,
    ln1_shift,
    w_query,
    b_query,
    w_key,
    w_value,
    b_value,
    w_out,
    b_out,
    ln2_gain,
    ln2_shift,
    w_up,
    b_up,
    w_down,
    b_down,
):
    heads_here = w_query.shape[1] // HEAD_DIM
    score_scale = 1.0 / math.sqrt(HEAD_DIM)
    positions = jnp.arange(SEQ, dtype=jnp.int32)
    sum_w_query = jnp.zeros(w_query.shape, jnp.float32)
    sum_b_query = jnp.zeros(b_query.shape, jnp.float32)
    sum_w_key = jnp.zeros(w_key.shape, jnp.float32)
    sum_w_value = jnp.zeros(w_value.shape, jnp.float32)
    sum_b_value = jnp.zeros(b_value.shape, jnp.float32)
    sum_w_out = jnp.zeros(w_out.shape, jnp.float32)
    sum_w_up = jnp.zeros(w_up.shape, jnp.float32)
    sum_b_up = jnp.zeros(b_up.shape, jnp.float32)
    sum_w_down = jnp.zeros(w_down.shape, jnp.float32)
    sum_ln1_gain = jnp.zeros(ln1_gain.shape, jnp.float32)
    sum_ln1_shift = jnp.zeros(ln1_shift.shape, jnp.float32)
    sum_ln2_gain = jnp.zeros(ln2_gain.shape, jnp.float32)
    sum_ln2_shift = jnp.zeros(ln2_shift.shape, jnp.float32)
    sum_b_out = jnp.zeros(b_out.shape, jnp.float32)
    sum_b_down = jnp.zeros(b_down.shape, jnp.float32)
    outputs = []
    input_grads = []
    for micro_idx in range(MB):
        row_start = micro_idx * ROWS_MB
        inputs = tokens[row_start : row_start + ROWS_MB].astype(jnp.float32)
        row_lengths = lengths[row_start : row_start + ROWS_MB]
        upstream = out_grad[row_start : row_start + ROWS_MB]
        normed_in, unit_in, inv_in = layer_norm(inputs, ln1_gain, ln1_shift)
        full_in = lax.all_gather(normed_in.astype(jnp.bfloat16), "mp", axis=1, tiled=True)
        rows_mb = full_in.shape[0]
        query_low = (
            (product("bsd,de->bse", full_in, w_query) + b_query)
            .astype(jnp.bfloat16)
            .reshape(rows_mb, SEQ, heads_here, HEAD_DIM)
        )
        keys_low = (
            product("bsd,de->bse", full_in, w_key)
            .astype(jnp.bfloat16)
            .reshape(rows_mb, SEQ, heads_here, HEAD_DIM)
        )
        values_low = (
            (product("bsd,de->bse", full_in, w_value) + b_value)
            .astype(jnp.bfloat16)
            .reshape(rows_mb, SEQ, heads_here, HEAD_DIM)
        )
        key_valid = (positions[None, :] < row_lengths[:, None])[:, None, None, :]
        scores = masked_scores(query_low, keys_low, key_valid, score_scale)
        row_max = jnp.max(scores, axis=-1, keepdims=True)
        log_total = row_max + jnp.log(jnp.sum(jnp.exp(scores - row_max), axis=-1, keepdims=True))
        prob_low = jnp.exp(scores - log_total).astype(jnp.bfloat16)
        mixed_low = (
            product("bhqk,bkhd->bqhd", prob_low, values_low)
            .reshape(rows_mb, SEQ, heads_here * HEAD_DIM)
            .astype(jnp.bfloat16)
        )
        attended = lax.psum_scatter(
            product("bse,ed->bsd", mixed_low, w_out), "mp", scatter_dimension=1, tiled=True
        )
        residual = inputs + attended + b_out
        normed_mid, unit_mid, inv_mid = layer_norm(residual, ln2_gain, ln2_shift)
        full_mid = lax.all_gather(normed_mid.astype(jnp.bfloat16), "mp", axis=1, tiled=True)
        hidden = product("bsd,df->bsf", full_mid, w_up) + b_up
        active = jax.nn.gelu(hidden, approximate=False).astype(jnp.bfloat16)
        branch = lax.psum_scatter(
            product("bsf,fd->bsd", active, w_down).astype(jnp.bfloat16),
            "mp",
            scatter_dimension=1,
            tiled=True,
        ).astype(jnp.float32)
        outputs.append((residual + branch + b_down).astype(jnp.bfloat16))
        grad_full = lax.all_gather(upstream, "mp", axis=1, tiled=True)
        upstream_f = upstream.astype(jnp.float32)
        sum_w_down = sum_w_down + product("bsf,bsd->fd", active, grad_full)
        sum_b_down = sum_b_down + token_sum(upstream_f)
        grad_hidden = (product("bsd,fd->bsf", grad_full, w_down) * gelu_slope(hidden)).astype(
            jnp.bfloat16
        )
        sum_w_up = sum_w_up + product("bsd,bsf->df", full_mid, grad_hidden)
        sum_b_up = sum_b_up + token_sum(grad_hidden.astype(jnp.float32))
        grad_norm_mid = lax.psum_scatter(
            product("bsf,df->bsd", grad_hidden, w_up), "mp", scatter_dimension=1, tiled=True
        )
        sum_ln2_gain = sum_ln2_gain + token_sum(grad_norm_mid * unit_mid)
        sum_ln2_shift = sum_ln2_shift + token_sum(grad_norm_mid)
        grad_residual = upstream_f + norm_back(grad_norm_mid, unit_mid, inv_mid, ln2_gain)
        sum_b_out = sum_b_out + token_sum(grad_residual)
        grad_attn = lax.all_gather(grad_residual.astype(jnp.bfloat16), "mp", axis=1, tiled=True)
        sum_w_out = sum_w_out + product("bse,bsd->ed", mixed_low, grad_attn)
        grad_mixed = (
            product("bsd,ed->bse", grad_attn, w_out)
            .astype(jnp.bfloat16)
            .reshape(rows_mb, SEQ, heads_here, HEAD_DIM)
        )
        grad_probs = product("bqhd,bkhd->bhqk", grad_mixed, values_low)
        probs_full = jnp.exp(masked_scores(query_low, keys_low, key_valid, score_scale) - log_total)
        row_delta = jnp.sum(probs_full * grad_probs, axis=-1, keepdims=True)
        grad_scores = (probs_full * (grad_probs - row_delta)).astype(jnp.bfloat16)
        grad_query = (
            (product("bhqk,bkhd->bqhd", grad_scores, keys_low) * score_scale)
            .astype(jnp.bfloat16)
            .reshape(rows_mb, SEQ, heads_here * HEAD_DIM)
        )
        grad_keys = (
            (product("bhqk,bqhd->bkhd", grad_scores, query_low) * score_scale)
            .astype(jnp.bfloat16)
            .reshape(rows_mb, SEQ, heads_here * HEAD_DIM)
        )
        grad_values = (
            product("bhqk,bqhd->bkhd", prob_low, grad_mixed)
            .astype(jnp.bfloat16)
            .reshape(rows_mb, SEQ, heads_here * HEAD_DIM)
        )
        sum_w_query = sum_w_query + product("bsd,bse->de", full_in, grad_query)
        sum_b_query = sum_b_query + token_sum(grad_query.astype(jnp.float32))
        sum_w_key = sum_w_key + product("bsd,bse->de", full_in, grad_keys)
        sum_w_value = sum_w_value + product("bsd,bse->de", full_in, grad_values)
        sum_b_value = sum_b_value + token_sum(grad_values.astype(jnp.float32))
        input_terms = (
            product("bse,de->bsd", grad_query, w_query)
            + product("bse,de->bsd", grad_keys, w_key)
            + product("bse,de->bsd", grad_values, w_value)
        )
        grad_norm_in = lax.psum_scatter(
            input_terms.astype(jnp.bfloat16), "mp", scatter_dimension=1, tiled=True
        ).astype(jnp.float32)
        sum_ln1_gain = sum_ln1_gain + token_sum(grad_norm_in * unit_in)
        sum_ln1_shift = sum_ln1_shift + token_sum(grad_norm_in)
        input_grads.append(grad_residual + norm_back(grad_norm_in, unit_in, inv_in, ln1_gain))
    totals = tuple(
        lax.psum(
            (
                sum_w_query,
                sum_b_query,
                sum_w_key,
                sum_w_value,
                sum_b_value,
                sum_w_out,
                sum_w_up,
                sum_b_up,
                sum_w_down,
            ),
            "dp",
        )
    )
    common = lax.psum(
        (sum_ln1_gain, sum_ln1_shift, sum_ln2_gain, sum_ln2_shift, sum_b_out, sum_b_down),
        ("dp", "mp"),
    )
    block_out = jnp.concatenate(outputs, axis=0)
    input_grad = jnp.concatenate(input_grads, axis=0)
    return (
        block_out,
        input_grad,
        common[0],
        common[1],
        totals[0],
        totals[1],
        totals[2],
        totals[3],
        totals[4],
        totals[5],
        common[4],
        common[2],
        common[3],
        totals[6],
        totals[7],
        totals[8],
        common[5],
    )


def solution(mesh):
    in_specs = (
        P("dp", "mp", None),
        P("dp"),
        P("dp", "mp", None),
        P(),
        P(),
        P(None, "mp"),
        P("mp"),
        P(None, "mp"),
        P(None, "mp"),
        P("mp"),
        P("mp", None),
        P(),
        P(),
        P(),
        P(None, "mp"),
        P("mp"),
        P("mp", None),
        P(),
    )
    out_specs = (
        P("dp", "mp", None),
        P("dp", "mp", None),
        P(),
        P(),
        P(None, "mp"),
        P("mp"),
        P(None, "mp"),
        P(None, "mp"),
        P("mp"),
        P("mp", None),
        P(),
        P(),
        P(),
        P(None, "mp"),
        P("mp"),
        P("mp", None),
        P(),
    )
    return jax.shard_map(
        on_device, mesh=mesh, in_specs=in_specs, out_specs=out_specs, check_vma=False
    )
```

profile of v0, /device:TPU:0, one launch (start us, length us, event | category | flops | bytes accessed | tf_op | source)
XLA Modules:
  0.0 931.7 jit_solution(8912068039627414131)
XLA Ops:
  12.2 12.8 %all_gather.52 = bf16[1,512,768]{2,1,0:T(8,128)(2,1)S(1)} all-gather(bf16[1,256,768]{2,1,0:T(8,128)(2,1)S(1)} %fusion.127), channel_id=1, replica_groups=mesh['dp'=16,'mp'=2] {'mp'}, dimensions={1}, use_global_device_ids=true | all-gather | bytes 1179648 | tf_op jit(solution)/shard_map/all_gather | solution.py:99
  40.5 16.8 %all_gather.60 = bf16[1,512,768]{2,1,0:T(8,128)(2,1)} all-gather(bf16[1,256,768]{2,1,0:T(8,128)(2,1)S(1)} %get-tuple-element.113), channel_id=1, replica_groups=mesh['dp'=16,'mp'=2] {'mp'}, dimensions={1}, use_global_device_ids=true | all-gather | bytes 1179648 | tf_op jit(solution)/shard_map/all_gather | solution.py:141
  57.3 12.3 %reduce-scatter.25.cloned.1.call-done = f32[1,256,768]{2,1,0:T(8,128)} async-done(((f32[1,512,768]{2,1,0:T(8,128)}), f32[1,256,768]{2,1,0:T(8,128)}) %reduce-scatter.25.cloned.1.call-update) | async-done | bytes 786448 | tf_op jit(solution)/shard_map/reduce_scatter | solution.py:126
  72.2 11.9 %all_gather.53 = bf16[1,512,768]{2,1,0:T(8,128)(2,1)S(1)} all-gather(bf16[1,256,768]{2,1,0:T(8,128)(2,1)S(1)} %add_convert_fusion.7), channel_id=1, replica_groups=mesh['dp'=16,'mp'=2] {'mp'}, dimensions={1}, use_global_device_ids=true | all-gather | bytes 1179648 | tf_op jit(solution)/shard_map/all_gather | solution.py:131
  84.1 10.3 %fusion.16 = (bf16[512,1536]{1,0:T(8,128)(2,1)}, f32[512,1536]{1,0:T(8,128)S(1)}) fusion(f32[1536]{0:T(1024)} %param.33, bf16[768,1536]{1,0:T(8,128)(2,1)S(1)} %copy-done, bf16[1,512,768]{2,1,0:T(8,128)(2,1)S(1)} %all_gather.53), kind=kOutput, calls=%fused_computation.54 | convolution fusion | flops 1259864064 | bytes 7870464 | tf_op jit(solution)/shard_map/bsd,df->bsf/dot_general | solution.py:41
  105.6 22.8 %reduce-scatter.41.cloned.1.call-done = f32[1,256,768]{2,1,0:T(8,128)} async-done(((f32[1,512,768]{2,1,0:T(8,128)}), f32[1,256,768]{2,1,0:T(8,128)}) %reduce-scatter.41.cloned.1.call-update) | async-done | bytes 786448 | tf_op jit(solution)/shard_map/reduce_scatter | solution.py:150
  131.1 17.6 %reduce-scatter.27.cloned.1.call-done = bf16[1,256,768]{2,1,0:T(8,128)(2,1)} async-done(((bf16[1,512,768]{2,1,0:T(8,128)(2,1)}), bf16[1,256,768]{2,1,0:T(8,128)(2,1)}) %reduce-scatter.27.cloned.1.call-update) | async-done | bytes 393232 | tf_op jit(solution)/shard_map/reduce_scatter | solution.py:134
  152.3 11.8 %all_gather.61 = bf16[1,512,768]{2,1,0:T(8,128)(2,1)S(1)} all-gather(bf16[1,256,768]{2,1,0:T(8,128)(2,1)S(1)} %convert_element_type.620), channel_id=1, replica_groups=mesh['dp'=16,'mp'=2] {'mp'}, dimensions={1}, use_global_device_ids=true | all-gather | bytes 1179648 | tf_op jit(solution)/shard_map/all_gather | solution.py:157
  180.8 15.7 %reduce-scatter.43.cloned.1.call-done = bf16[1,256,768]{2,1,0:T(8,128)(2,1)} async-done(((bf16[1,512,768]{2,1,0:T(8,128)(2,1)}), bf16[1,256,768]{2,1,0:T(8,128)(2,1)}) %reduce-scatter.43.cloned.1.call-update) | async-done | bytes 393232 | tf_op jit(solution)/shard_map/reduce_scatter | solution.py:193
  202.1 11.9 %all_gather.54 = bf16[1,512,768]{2,1,0:T(8,128)(2,1)S(1)} all-gather(bf16[1,256,768]{2,1,0:T(8,128)(2,1)S(1)} %get-tuple-element.97), channel_id=1, replica_groups=mesh['dp'=16,'mp'=2] {'mp'}, dimensions={1}, use_global_device_ids=true | all-gather | bytes 1179648 | tf_op jit(solution)/shard_map/all_gather | solution.py:99
  227.7 17.3 %all_gather.50 = bf16[1,512,768]{2,1,0:T(8,128)(2,1)S(1)} all-gather(bf16[1,256,768]{2,1,0:T(8,128)(2,1)} %get-tuple-element.96), channel_id=1, replica_groups=mesh['dp'=16,'mp'=2] {'mp'}, dimensions={1}, use_global_device_ids=true | all-gather | bytes 1179648 | tf_op jit(solution)/shard_map/all_gather | solution.py:99
  259.8 10.1 %all_gather.48 = bf16[1,512,768]{2,1,0:T(8,128)(2,1)S(1)} all-gather(bf16[1,256,768]{2,1,0:T(8,128)(2,1)} %get-tuple-element.95), channel_id=1, replica_groups=mesh['dp'=16,'mp'=2] {'mp'}, dimensions={1}, use_global_device_ids=true | all-gather | bytes 1179648 | tf_op jit(solution)/shard_map/all_gather | solution.py:99
  284.0 10.0 %all_gather.62 = bf16[1,512,768]{2,1,0:T(8,128)(2,1)} all-gather(bf16[1,256,768]{2,1,0:T(8,128)(2,1)} %get-tuple-element.112), channel_id=1, replica_groups=mesh['dp'=16,'mp'=2] {'mp'}, dimensions={1}, use_global_device_ids=true | all-gather | bytes 1179648 | tf_op jit(solution)/shard_map/all_gather | solution.py:141
  294.0 18.5 %all_gather.58 = bf16[1,512,768]{2,1,0:T(8,128)(2,1)} all-gather(bf16[1,256,768]{2,1,0:T(8,128)(2,1)} %get-tuple-element.111), channel_id=1, replica_groups=mesh['dp'=16,'mp'=2] {'mp'}, dimensions={1}, use_global_device_ids=true | all-gather | bytes 1179648 | tf_op jit(solution)/shard_map/all_gather | solution.py:141
  312.5 15.9 %all_gather.56 = bf16[1,512,768]{2,1,0:T(8,128)(2,1)} all-gather(bf16[1,256,768]{2,1,0:T(8,128)(2,1)S(1)} %copy-done.115), channel_id=1, replica_groups=mesh['dp'=16,'mp'=2] {'mp'}, dimensions={1}, use_global_device_ids=true | all-gather | bytes 1179648 | tf_op jit(solution)/shard_map/all_gather | solution.py:141
  332.5 11.9 %all_gather.55 = bf16[1,512,768]{2,1,0:T(8,128)(2,1)} all-gather(bf16[1,256,768]{2,1,0:T(8,128)(2,1)S(1)} %get-tuple-element.120), channel_id=1, replica_groups=mesh['dp'=16,'mp'=2] {'mp'}, dimensions={1}, use_global_device_ids=true | all-gather | bytes 1179648 | tf_op jit(solution)/shard_map/all_gather | solution.py:131
  344.3 10.9 %all_gather.51 = bf16[1,512,768]{2,1,0:T(8,128)(2,1)S(1)} all-gather(bf16[1,256,768]{2,1,0:T(8,128)(2,1)S(1)} %get-tuple-element.119), channel_id=1, replica_groups=mesh['dp'=16,'mp'=2] {'mp'}, dimensions={1}, use_global_device_ids=true | all-gather | bytes 1179648 | tf_op jit(solution)/shard_map/all_gather | solution.py:131
  355.2 9.4 %fusion.13 = (bf16[512,1536]{1,0:T(8,128)(2,1)}, f32[512,1536]{1,0:T(8,128)S(1)}) fusion(f32[1536]{0:T(1024)S(1)} %copy-done.189, bf16[768,1536]{1,0:T(8,128)(2,1)S(1)} %copy-done, bf16[1,512,768]{2,1,0:T(8,128)(2,1)S(1)} %all_gather.51), kind=kOutput, calls=%fused_computation.51 | convolution fusion | flops 1259864064 | bytes 7870464 | tf_op jit(solution)/shard_map/bsd,df->bsf/dot_general | solution.py:41
  364.7 10.3 %all_gather.49 = bf16[1,512,768]{2,1,0:T(8,128)(2,1)} all-gather(bf16[1,256,768]{2,1,0:T(8,128)(2,1)S(1)} %get-tuple-element.118), channel_id=1, replica_groups=mesh['dp'=16,'mp'=2] {'mp'}, dimensions={1}, use_global_device_ids=true | all-gather | bytes 1179648 | tf_op jit(solution)/shard_map/all_gather | solution.py:131
  381.6 9.8 %fusion.19 = (bf16[512,1536]{1,0:T(8,128)(2,1)}, f32[512,1536]{1,0:T(8,128)S(1)}) fusion(f32[1536]{0:T(1024)S(1)} %copy-done.189, bf16[768,1536]{1,0:T(8,128)(2,1)S(1)} %copy-done, bf16[1,512,768]{2,1,0:T(8,128)(2,1)} %all_gather.55), kind=kOutput, calls=%fused_computation.57 | convolution fusion | flops 1259864064 | bytes 7870464 | tf_op jit(solution)/shard_map/bsd,df->bsf/dot_general | solution.py:41
  398.6 9.8 %fusion.10 = (bf16[512,1536]{1,0:T(8,128)(2,1)}, f32[512,1536]{1,0:T(8,128)S(1)}) fusion(f32[1536]{0:T(1024)S(1)} %copy-done.189, bf16[768,1536]{1,0:T(8,128)(2,1)S(1)} %copy-done, bf16[1,512,768]{2,1,0:T(8,128)(2,1)} %all_gather.49), kind=kOutput, calls=%fused_computation.48 | convolution fusion | flops 1259864064 | bytes 7870464 | tf_op jit(solution)/shard_map/bsd,df->bsf/dot_general | solution.py:41
  419.9 5.4 fusion.162
  450.1 9.8 %add_add_fusion = f32[1536,768]{1,0:T(8,128)} fusion(f32[1536,768]{1,0:T(8,128)} %fusion.162, f32[1536,768]{1,0:T(8,128)} %fusion.173, f32[1536,768]{1,0:T(8,128)} %fusion.167, bf16[512,1536]{1,0:T(8,128)(2,1)} %get-tuple-element.145, bf16[1,512,768]{2,1,0:T(8,128)(2,1)} %all_gather.62), kind=kOutput, calls=%fused_computation.32 | convolution fusion | flops 1211498496 | bytes 21233664 | tf_op jit(solution)/shard_map/bsf,bsd->fd/dot_general | solution.py:41
  459.9 9.1 add_add_fusion.1
  472.7 12.7 %reduce-scatter.19.cloned.1.call-done = bf16[1,256,768]{2,1,0:T(8,128)(2,1)} async-done(((bf16[1,512,768]{2,1,0:T(8,128)(2,1)}), bf16[1,256,768]{2,1,0:T(8,128)(2,1)}) %reduce-scatter.19.cloned.1.call-update) | async-done | bytes 393232 | tf_op jit(solution)/shard_map/reduce_scatter | solution.py:134
  485.4 20.2 %reduce-scatter.31.cloned.1.call-done = bf16[1,256,768]{2,1,0:T(8,128)(2,1)} async-done(((bf16[1,512,768]{2,1,0:T(8,128)(2,1)}), bf16[1,256,768]{2,1,0:T(8,128)(2,1)}) %reduce-scatter.31.cloned.1.call-update) | async-done | bytes 393232 | tf_op jit(solution)/shard_map/reduce_scatter | solution.py:134
  510.7 19.0 %all_gather.57 = bf16[1,512,768]{2,1,0:T(8,128)(2,1)S(1)} all-gather(bf16[1,256,768]{2,1,0:T(8,128)(2,1)S(1)} %convert_element_type.586), channel_id=1, replica_groups=mesh['dp'=16,'mp'=2] {'mp'}, dimensions={1}, use_global_device_ids=true | all-gather | bytes 1179648 | tf_op jit(solution)/shard_map/all_gather | solution.py:157
  546.8 8.5 all_gather.59
  567.0 8.9 all_gather.63
  641.6 60.4 %all-reduce.1 = (f32[384]{0:T(512)}, f32[384]{0:T(512)}, f32[1536]{0:T(1024)}) all-reduce(f32[384]{0:T(512)} %add.700, f32[384]{0:T(512)} %add.710, f32[1536]{0:T(1024)S(1)} %add_add_fusion.2), channel_id=1, replica_groups=mesh['dp'=16,'mp'=2] {'dp'}, use_global_device_ids=true, to_apply=%region_75.76 | all-reduce | flops 2304 | bytes 18432 | tf_op jit(solution)/shard_map/psum | solution.py:200
  712.5 39.4 %all-reduce = (f32[768]{0:T(1024)}, f32[768]{0:T(1024)}, f32[768]{0:T(1024)}, f32[768]{0:T(1024)}, f32[768]{0:T(1024)}, /*index=5*/f32[768]{0:T(1024)}) all-reduce(f32[768]{0:T(1024)} %add_add_fusion.10, f32[768]{0:T(1024)} %add_add_fusion.9, f32[768]{0:T(1024)} %add_add_fusion.6, ...), channel_id=1, replica_groups=mesh['dp'=16,'mp'=2] {'dp','mp'}, use_global_device_ids=true, to_apply=%region_64.65 | all-reduce | flops 4608 | bytes 36864 | tf_op jit(solution)/shard_map/psum | solution.py:215
  762.3 151.8 %all-reduce.5.cloned.1.call-done = (f32[768,384]{1,0:T(8,128)}, f32[768,384]{1,0:T(8,128)}, f32[768,384]{1,0:T(8,128)}, f32[384,768]{1,0:T(8,128)}, f32[768,1536]{1,0:T(8,128)}, /*index=5*/f32[1536,768]{1,0:T(8,128)}) async-done(((f32[768,384]{1,0:T(8,128)}, f32[768,384]{1,0:T(8,128)}, f32[768,384]{1,0:T(8,128)}, f32[384,768]{1,0:T(8,128)}, f32[768,1536]{1,0:T(8,128)}, /*index=5*/f32[1536,768]{1,0:T(8,128)}), ...) | async-done | bytes 14155792 | tf_op jit(solution)/shard_map/psum | solution.py:200
  (646 shorter events, 292.2 us)
Async XLA Ops:
  7.2 76.9 %copy-start = (bf16[768,1536]{1,0:T(8,128)(2,1)S(1)}, bf16[768,1536]{1,0:T(8,128)(2,1)}, u32[]{:S(2)}) copy-start(bf16[768,1536]{1,0:T(8,128)(2,1)} %param.32) | copy-start | bytes 7077892
  7.2 62.3 %reduce-scatter.25.cloned.1.call-start = ((), (), s32[]{:S(2)}) async-start(), calls=%async_computation.20 | async-start | bytes 2359296 | tf_op jit(solution)/shard_map/reduce_scatter | solution.py:126
  38.0 90.4 %reduce-scatter.41.cloned.1.call-start = ((), (), s32[]{:S(2)}) async-start(), calls=%async_computation.28 | async-start | bytes 2359296 | tf_op jit(solution)/shard_map/reduce_scatter | solution.py:150
  101.0 47.7 %reduce-scatter.27.cloned.1.call-start = ((), (), s32[]{:S(2)}) async-start(), calls=%async_computation.21 | async-start | bytes 1179648 | tf_op jit(solution)/shard_map/reduce_scatter | solution.py:134
  105.5 91.0 %reduce-scatter.43.cloned.1.call-start = ((), (), s32[]{:S(2)}) async-start(), calls=%async_computation.29 | async-start | bytes 1179648 | tf_op jit(solution)/shard_map/reduce_scatter | solution.py:193
  178.9 149.6 %reduce-scatter.29.cloned.1.call-start = ((), (), s32[]{:S(2)}) async-start(), calls=%async_computation.22 | async-start | bytes 2359296 | tf_op jit(solution)/shard_map/reduce_scatter | solution.py:126
  180.1 35.1 %copy-start.144 = (f32[256]{0:T(256)}, f32[256]{0:T(256)S(1)}, u32[]{:S(2)}) copy-start(f32[256]{0:T(256)S(1)} %broadcast_multiply_fusion.17) | copy-start | bytes 3076
  180.8 34.4 %copy-start.148 = (f32[256]{0:T(256)}, f32[256]{0:T(256)S(1)}, u32[]{:S(2)}) copy-start(f32[256]{0:T(256)S(1)} %get-tuple-element.182) | copy-start | bytes 3076
  226.9 101.5 %reduce-scatter.21.cloned.1.call-start = ((), (), s32[]{:S(2)}) async-start(), calls=%async_computation.18 | async-start | bytes 2359296 | tf_op jit(solution)/shard_map/reduce_scatter | solution.py:126
  259.0 69.8 %reduce-scatter.17.cloned.1.call-start = ((), (), s32[]{:S(2)}) async-start(), calls=%async_computation.16 | async-start | bytes 2359296 | tf_op jit(solution)/shard_map/reduce_scatter | solution.py:126
  283.9 44.9 %copy-start.166 = (f32[768]{0:T(1024)S(1)}, f32[768]{0:T(1024)}, u32[]{:S(2)}) copy-start(f32[768]{0:T(1024)} %param.29) | copy-start | bytes 9220
  284.0 185.0 %reduce-scatter.37.cloned.1.call-start = ((), (), s32[]{:S(2)}) async-start(), calls=%async_computation.26 | async-start | bytes 2359296 | tf_op jit(solution)/shard_map/reduce_scatter | solution.py:150
  331.5 137.5 %copy-start.146 = (f32[256]{0:T(256)}, f32[256]{0:T(256)S(1)}, u32[]{:S(2)}) copy-start(f32[256]{0:T(256)S(1)} %broadcast_multiply_fusion.20) | copy-start | bytes 3076
  331.7 137.3 %copy-start.172 = (f32[256]{0:T(256)}, f32[256]{0:T(256)S(1)}, u32[]{:S(2)}) copy-start(f32[256]{0:T(256)S(1)} %add_rsqrt_fusion.4) | copy-start | bytes 3076
  381.6 87.4 %reduce-scatter.45.cloned.1.call-start = ((), (), s32[]{:S(2)}) async-start(), calls=%async_computation.30 | async-start | bytes 2359296 | tf_op jit(solution)/shard_map/reduce_scatter | solution.py:150
  398.1 70.9 %reduce-scatter.33.cloned.1.call-start = ((), (), s32[]{:S(2)}) async-start(), calls=%async_computation.24 | async-start | bytes 2359296 | tf_op jit(solution)/shard_map/reduce_scatter | solution.py:150
  415.0 70.5 %reduce-scatter.19.cloned.1.call-start = ((), (), s32[]{:S(2)}) async-start(), calls=%async_computation.17 | async-start | bytes 1179648 | tf_op jit(solution)/shard_map/reduce_scatter | solution.py:134
  419.8 85.8 %reduce-scatter.31.cloned.1.call-start = ((), (), s32[]{:S(2)}) async-start(), calls=%async_computation.23 | async-start | bytes 1179648 | tf_op jit(solution)/shard_map/reduce_scatter | solution.py:134
  434.8 108.7 %reduce-scatter.23.cloned.1.call-start = ((), (), s32[]{:S(2)}) async-start(), calls=%async_computation.19 | async-start | bytes 1179648 | tf_op jit(solution)/shard_map/reduce_scatter | solution.py:134
  450.0 256.3 %reduce-scatter.35.cloned.1.call-start = ((), (), s32[]{:S(2)}) async-start(), calls=%async_computation.25 | async-start | bytes 1179648 | tf_op jit(solution)/shard_map/reduce_scatter | solution.py:193
  468.9 36.7 %copy-start.142 = (f32[768]{0:T(1024)S(1)}, f32[768]{0:T(1024)}, u32[]{:S(2)}) copy-start(f32[768]{0:T(1024)} %param.35) | copy-start | bytes 9220
  587.9 118.4 %reduce-scatter.39.cloned.1.call-start = ((), (), s32[]{:S(2)}) async-start(), calls=%async_computation.27 | async-start | bytes 1179648 | tf_op jit(solution)/shard_map/reduce_scatter | solution.py:193
  608.4 98.0 %reduce-scatter.47.cloned.1.call-start = ((), (), s32[]{:S(2)}) async-start(), calls=%async_computation.31 | async-start | bytes 1179648 | tf_op jit(solution)/shard_map/reduce_scatter | solution.py:193
  622.8 291.3 %all-reduce.5.cloned.1.call-start = ((), (), s32[]{:S(2)}) async-start(), calls=%async_computation.32 | async-start | bytes 28311552 | tf_op jit(solution)/shard_map/psum | solution.py:200
  631.1 71.0 %copy-start.105 = (bf16[1,256,768]{2,1,0:T(8,128)(2,1)S(1)}, bf16[1,256,768]{2,1,0:T(8,128)(2,1)}, u32[]{:S(2)}) copy-start(bf16[1,256,768]{2,1,0:T(8,128)(2,1)} %get-tuple-element.114) | copy-start | bytes 1179652
  631.1 71.0 %copy-start.112 = (bf16[1,256,768]{2,1,0:T(8,128)(2,1)S(1)}, bf16[1,256,768]{2,1,0:T(8,128)(2,1)}, u32[]{:S(2)}) copy-start(bf16[1,256,768]{2,1,0:T(8,128)(2,1)} %get-tuple-element.117) | copy-start | bytes 1179652
  631.1 71.0 %copy-start.116 = (bf16[1,256,768]{2,1,0:T(8,128)(2,1)S(1)}, bf16[1,256,768]{2,1,0:T(8,128)(2,1)}, u32[]{:S(2)}) copy-start(bf16[1,256,768]{2,1,0:T(8,128)(2,1)} %get-tuple-element.115) | copy-start | bytes 1179652
  631.2 75.2 %copy-start.141 = (f32[768]{0:T(1024)S(1)}, f32[768]{0:T(1024)}, u32[]{:S(2)}) copy-start(f32[768]{0:T(1024)} %param.21) | copy-start | bytes 9220
  631.2 75.2 %copy-start.145 = (f32[256]{0:T(256)S(1)}, f32[256]{0:T(256)}, u32[]{:S(2)}) copy-start(f32[256]{0:T(256)} %copy-done.144) | copy-start | bytes 3076
  706.3 52.7 %copy-start.44 = (f32[1,256,768]{2,1,0:T(8,128)S(1)}, f32[1,256,768]{2,1,0:T(8,128)}, u32[]{:S(2)}) copy-start(f32[1,256,768]{2,1,0:T(8,128)} %copy-done.43) | copy-start | bytes 2359300
  706.3 52.7 %copy-start.150 = (f32[256]{0:T(256)S(1)}, f32[256]{0:T(256)}, u32[]{:S(2)}) copy-start(f32[256]{0:T(256)} %copy-done.149) | copy-start | bytes 3076
  706.4 52.7 %copy-start.117 = (bf16[1,256,768]{2,1,0:T(8,128)(2,1)S(1)}, bf16[1,256,768]{2,1,0:T(8,128)(2,1)}, u32[]{:S(2)}) copy-start(bf16[1,256,768]{2,1,0:T(8,128)(2,1)} %reduce-scatter.47.cloned.1.call-done) | copy-start | bytes 1179652
  (191 other events, 1233.2 us)
Sparse Core Ops, SparseCore 0:
  38.1 31.3 reduce-scatter.24
  101.1 27.2 reduce-scatter.40
  131.2 17.4 reduce-scatter.26
  179.0 17.4 reduce-scatter.42
  227.0 30.0 reduce-scatter.28
  259.9 29.3 reduce-scatter.20
  292.1 36.6 reduce-scatter.16
  381.7 26.7 reduce-scatter.36
  410.8 26.0 reduce-scatter.44
  439.1 26.0 reduce-scatter.32
  468.0 17.4 reduce-scatter.18
  488.2 17.4 reduce-scatter.30
  508.5 23.4 reduce-scatter.22
  588.0 17.4 reduce-scatter.34
  608.5 17.4 reduce-scatter.38
  628.7 17.4 reduce-scatter.46
  652.3 261.7 all-reduce.4
where the time goes:
time: 940 us; the launch traced here: 932 us
  blocking collectives  306 us (33%)
  waiting for transfers between devices  254 us (27%)
  matrix products  229 us (24%)
  other arithmetic  87.3 us (9%)
  local copies, waits for them, and re-layouts  37.1 us (4%)
  between operations  16.5 us (2%)
    dot_general x96, matrix products, product(): jnp.einsum(pattern, left_side, right_side, preferred_element_type=jnp.flo...  229 us
    psum x1, waiting for transfers between devices, on_device(): lax.psum((sum_w_query, sum_b_query, sum_w_key, sum_w_value, sum_b_value,...  152 us
    all_gather x4, blocking collectives, on_device(): grad_full = lax.all_gather(upstream, 'mp', axis=1, tiled=True)  61.2 us
    psum x1, blocking collectives, on_device(): lax.psum((sum_w_query, sum_b_query, sum_w_key, sum_w_value, sum_b_value,...  60.4 us
    all_gather x4, blocking collectives, on_device(): lax.all_gather(normed_in.astype(jnp.bfloat16), 'mp', axis=1, tiled=True)  52 us
    reduce_scatter x4, waiting for transfers between devices, on_device(): lax.psum_scatter(product('bsf,fd->bsd', active, w_down).astype(jnp.bfloat...  50.5 us
    all_gather x4, blocking collectives, on_device(): lax.all_gather(grad_residual.astype(jnp.bfloat16), 'mp', axis=1, tiled=True)  48.1 us
    all_gather x4, blocking collectives, on_device(): lax.all_gather(normed_mid.astype(jnp.bfloat16), 'mp', axis=1, tiled=True)  45 us
  transfers between devices with their start and end apart: 17, of which 8 were waited for; matrix products, arithmetic and copies ran while one was open for 23% of the time, Pallas kernels for 0%

commit v1 on v0

v1 whole, which is shorter than its diff:
```python
import functools
import math

import jax
import jax.numpy as jnp
from jax import lax
from jax.experimental import pallas as pl
from jax.experimental.pallas import tpu as pltpu
from jax.sharding import Mesh
from jax.sharding import PartitionSpec as P

HEAD_DIM = 64
PAIR = 2 * HEAD_DIM
EPS = 1e-12
FILL = -1000000000.0
SCALE = 1.0 / math.sqrt(HEAD_DIM)
LOG2E = math.log2(math.e)
F32 = jnp.float32
BF16 = jnp.bfloat16
NT = (((1,), (1,)), ((), ()))
NN = (((1,), (0,)), ((), ()))
TN = (((0,), (0,)), ((), ()))


def mm(a, b, dims=NN):
    return lax.dot_general(a, b, dims, preferred_element_type=F32)


def key_mask(info, row, shape):
    seq = shape[0]
    slot = lax.broadcasted_iota(jnp.int32, shape, 0) + info[0]
    position = jnp.where(slot >= seq, slot - seq, slot)
    return position < info[1 + row]


def head_lanes(value, head):
    lane = lax.broadcasted_iota(jnp.int32, value.shape, 1)
    keep = lane < HEAD_DIM if head == 0 else lane >= HEAD_DIM
    return jnp.where(keep, value, jnp.zeros_like(value))


def attend_kernel(info, q_ref, k_ref, v_ref, o_ref, lse_ref):
    row = pl.program_id(0)
    q, k, v = q_ref[0], k_ref[0], v_ref[0]
    valid = key_mask(info, row, (k.shape[0], q.shape[0]))
    v_t = v.T
    parts = []
    for head in range(2):
        scores = mm(head_lanes(k, head), q, NT) * (SCALE * LOG2E)
        scores = jnp.where(valid, scores, FILL * LOG2E)
        top = jnp.max(scores, axis=0, keepdims=True)
        weight = jnp.exp2(scores - top)
        total = jnp.sum(weight, axis=0, keepdims=True)
        lse_ref[0, 0, head : head + 1, :] = top + jnp.log2(total)
        probs = (weight * (1.0 / total)).astype(BF16)
        parts.append(mm(v_t[head * HEAD_DIM : (head + 1) * HEAD_DIM], probs))
    o_ref[0] = jnp.concatenate(parts, axis=0).T.astype(BF16)


def attend_back_kernel(info, q_ref, k_ref, v_ref, do_ref, lse_ref, d_ref):
    row = pl.program_id(0)
    pair = pl.program_id(1)
    n_pairs = pl.num_programs(1)
    q, k, v, do = q_ref[0], k_ref[0], v_ref[0], do_ref[0]
    valid = key_mask(info, row, (k.shape[0], q.shape[0]))
    k_t = k.T
    dq_t, dk, dv = [], [], []
    for head in range(2):
        scores = mm(head_lanes(k, head), q, NT) * (SCALE * LOG2E)
        scores = jnp.where(valid, scores, FILL * LOG2E)
        probs = jnp.exp2(scores - lse_ref[0, 0, head : head + 1, :])
        dv.append(mm(probs.astype(BF16), do))
        dprobs = mm(head_lanes(v, head), do, NT)
        delta = jnp.sum(probs * dprobs, axis=0, keepdims=True)
        dscores = (probs * (dprobs - delta)).astype(BF16)
        dk.append(mm(dscores, q))
        dq_t.append(mm(k_t[head * HEAD_DIM : (head + 1) * HEAD_DIM], dscores))
    first = lax.broadcasted_iota(jnp.int32, dv[0].shape, 1) < HEAD_DIM
    dq = jnp.concatenate(dq_t, axis=0).T * SCALE

    def put(slot, value):
        start = pl.multiple_of((slot * n_pairs + pair) * PAIR, PAIR)
        d_ref[0, :, pl.ds(start, PAIR)] = value.astype(BF16)

    put(0, dq)
    put(1, jnp.where(first, dk[0], dk[1]) * SCALE)
    put(2, jnp.where(first, dv[0], dv[1]))


def attend_specs(seq, n_pairs):
    return [
        pl.BlockSpec((1, seq, PAIR), lambda r, p, info: (r, 0, p)),
        pl.BlockSpec((1, seq, PAIR), lambda r, p, info: (r, 0, n_pairs + p)),
        pl.BlockSpec((1, seq, PAIR), lambda r, p, info: (r, 0, 2 * n_pairs + p)),
    ]


VMEM_LIMIT = 50 * 1024 * 1024


def attend(info, qkv):
    rows, seq, width = qkv.shape
    n_pairs = width // (3 * PAIR)
    flops = rows * n_pairs * 2 * 4 * seq * seq * HEAD_DIM
    return pl.pallas_call(
        attend_kernel,
        out_shape=(
            jax.ShapeDtypeStruct((rows, seq, n_pairs * PAIR), BF16),
            jax.ShapeDtypeStruct((rows, n_pairs, 2, seq), F32),
        ),
        grid_spec=pltpu.PrefetchScalarGridSpec(
            num_scalar_prefetch=1,
            grid=(rows, n_pairs),
            in_specs=attend_specs(seq, n_pairs),
            out_specs=(
                pl.BlockSpec((1, seq, PAIR), lambda r, p, info: (r, 0, p)),
                pl.BlockSpec((1, 1, 2, seq), lambda r, p, info: (r, p, 0, 0)),
            ),
        ),
        compiler_params=pltpu.CompilerParams(vmem_limit_bytes=VMEM_LIMIT),
        cost_estimate=pl.CostEstimate(
            flops=4 * flops,
            bytes_accessed=rows * seq * width * 4,
            transcendentals=rows * n_pairs * 2 * seq * seq,
        ),
        name="attend",
    )(info, qkv, qkv, qkv)


def attend_back(info, qkv, grad_mixed, lse):
    rows, seq, width = qkv.shape
    n_pairs = width // (3 * PAIR)
    flops = rows * n_pairs * 2 * 10 * seq * seq * HEAD_DIM
    return pl.pallas_call(
        attend_back_kernel,
        out_shape=jax.ShapeDtypeStruct((rows, seq, width), BF16),
        grid_spec=pltpu.PrefetchScalarGridSpec(
            num_scalar_prefetch=1,
            grid=(rows, n_pairs),
            in_specs=attend_specs(seq, n_pairs)
            + [
                pl.BlockSpec((1, seq, PAIR), lambda r, p, info: (r, 0, p)),
                pl.BlockSpec((1, 1, 2, seq), lambda r, p, info: (r, p, 0, 0)),
            ],
            out_specs=pl.BlockSpec((1, seq, width), lambda r, p, info: (r, 0, 0)),
        ),
        compiler_params=pltpu.CompilerParams(vmem_limit_bytes=VMEM_LIMIT),
        cost_estimate=pl.CostEstimate(
            flops=4 * flops,
            bytes_accessed=rows * seq * width * 6,
            transcendentals=rows * n_pairs * 2 * seq * seq,
        ),
        name="attend_back",
    )(info, qkv, qkv, qkv, grad_mixed, lse)


def ffn_kernel(first, *refs):
    if first:
        nm, nm_t, up, wu, wd, bu, y, gnm, gwu, gwd, gbu = refs
    else:
        nm, nm_t, up, wu, wd, bu, y_in, gnm_in, y, gnm, gwu, gwd, gbu = refs
    step = pl.program_id(0)

    @pl.when(step == 0)
    def _():
        if first:
            y[...] = jnp.zeros_like(y)
            gnm[...] = jnp.zeros_like(gnm)
        else:
            y[...] = y_in[...]
            gnm[...] = gnm_in[...]

    x, g = nm[...], up[...]
    w_up, w_down = wu[...], wd[...]
    hidden = mm(x, w_up) + bu[...]
    cdf = 0.5 * (1.0 + lax.erf(hidden * (1.0 / math.sqrt(2.0))))
    active = (hidden * cdf).astype(BF16)
    slope = cdf + hidden * jnp.exp(-0.5 * hidden * hidden) * (1.0 / math.sqrt(2.0 * math.pi))
    grad_hidden = (mm(g, w_down, NT) * slope).astype(BF16)
    gbu[...] = jnp.sum(grad_hidden.astype(F32), axis=0, keepdims=True)
    y[...] += mm(active, w_down)
    gwd[...] = mm(active, g, TN).astype(BF16)
    gnm[...] += mm(grad_hidden, w_up, NT)
    gwu[...] = mm(nm_t[...], grad_hidden).astype(BF16)


def ffn(nm, nm_t, up, wu, wd, bu, sums=None, block=256):
    tokens, width = nm.shape
    units = wu.shape[1]
    first = sums is None
    whole = lambda shape: pl.BlockSpec(shape, lambda f: (0, 0))
    once = lambda shape: pl.BlockSpec(shape, lambda f: (0, 0), pipeline_mode=pl.Buffered(1))
    in_specs = [
        once((tokens, width)),
        once((width, tokens)),
        once((tokens, width)),
        pl.BlockSpec((width, block), lambda f: (0, f)),
        pl.BlockSpec((block, width), lambda f: (f, 0)),
        pl.BlockSpec((1, block), lambda f: (0, f)),
    ]
    args = [nm, nm_t, up, wu, wd, bu]
    aliases = {}
    if not first:
        in_specs += [once((tokens, width))] * 2
        args += list(sums)
        aliases = {6: 0, 7: 1}
    return pl.pallas_call(
        functools.partial(ffn_kernel, first),
        out_shape=(
            jax.ShapeDtypeStruct((tokens, width), F32),
            jax.ShapeDtypeStruct((tokens, width), F32),
            jax.ShapeDtypeStruct((width, units), BF16),
            jax.ShapeDtypeStruct((units, width), BF16),
            jax.ShapeDtypeStruct((1, units), F32),
        ),
        grid=(units // block,),
        in_specs=in_specs,
        out_specs=(
            whole((tokens, width)),
            whole((tokens, width)),
            pl.BlockSpec((width, block), lambda f: (0, f)),
            pl.BlockSpec((block, width), lambda f: (f, 0)),
            pl.BlockSpec((1, block), lambda f: (0, f)),
        ),
        input_output_aliases=aliases,
        compiler_params=pltpu.CompilerParams(vmem_limit_bytes=VMEM_LIMIT),
        cost_estimate=pl.CostEstimate(
            flops=12 * tokens * width * units,
            bytes_accessed=tokens * width * 30 + 8 * width * units,
            transcendentals=2 * tokens * units,
        ),
        name="ffn_first" if first else "ffn_second",
    )(*args)


def norm(values):
    average = jnp.mean(values, axis=-1, keepdims=True)
    centred = values - average
    inv = lax.rsqrt(jnp.mean(centred * centred, axis=-1, keepdims=True) + EPS)
    return centred * inv, inv


def norm_back(grad, unit, inv, gain):
    scaled = grad * gain
    return inv * (
        scaled
        - jnp.mean(scaled, axis=-1, keepdims=True)
        - unit * jnp.mean(scaled * unit, axis=-1, keepdims=True)
    )


def swap(value, axis):
    return lax.ppermute(value, axis, [(0, 1), (1, 0)])


def part(value, index, count):
    size = value.shape[0] // count
    return lax.dynamic_slice_in_dim(value, index * size, size, 0)


def join(index, mine, other):
    return jnp.where(index == 0, jnp.concatenate([mine, other]), jnp.concatenate([other, mine]))


def fetch_half(weight):
    core = lax.axis_index("core")
    mine = swap(part(weight, core, 2), "mp")
    return join(core, mine, swap(mine, "core"))


def reduce_pieces(own, other):
    core = lax.axis_index("core")
    got_other = swap(part(other, 1 - core, 2), "core")
    mid_other = (part(other, core, 2).astype(F32) + got_other.astype(F32)).astype(BF16)
    got = swap(mid_other, "mp")
    got_own = swap(part(own, 1 - core, 2), "core")
    mid_own = part(own, core, 2).astype(F32) + got_own.astype(F32)
    return (mid_own + got.astype(F32)).astype(BF16)


def spread_pieces(piece):
    core = lax.axis_index("core")
    return join(core, piece, swap(piece, "core")).astype(F32)


def on_device(
    sizes,
    tokens,
    lengths,
    out_grad,
    ln1_gain,
    ln1_shift,
    w_query,
    b_query,
    w_key,
    w_value,
    b_value,
    w_out,
    b_out,
    ln2_gain,
    ln2_shift,
    w_up,
    b_up,
    w_down,
    b_down,
):
    side = lax.axis_index("mp")
    rows_dev, half, width = tokens.shape
    rows = rows_dev // 2
    seq = 2 * half
    total = rows * seq
    heads_width = w_query.shape[1]

    def take_rows(value):
        return jnp.concatenate([part(value, side, 2), swap(part(value, 1 - side, 2), "mp")], axis=1)

    x = take_rows(tokens).astype(F32).reshape(total, width)
    bias_own = jnp.concatenate([b_query, b_value, b_up])
    bias_oth = swap(bias_own, "mp")
    wqkv_own = jnp.concatenate([w_query, w_key, w_value], axis=1)
    wqkv_oth = fetch_half(wqkv_own)
    wout_oth = fetch_half(w_out)
    up = take_rows(out_grad).reshape(total, width)
    wup_oth = fetch_half(w_up)
    wdown_oth = fetch_half(w_down)
    info = jnp.concatenate([(side * half)[None].astype(jnp.int32), part(lengths, side, 2)])

    unit_in, inv_in = norm(x)
    normed_in = (unit_in * ln1_gain + ln1_shift).astype(BF16)

    def project(weight, bias):
        no_key = jnp.zeros((heads_width,), F32)
        full = jnp.concatenate([bias[:heads_width], no_key, bias[heads_width : 2 * heads_width]])
        return (mm(normed_in, weight) + full).astype(BF16).reshape(rows, seq, 3 * heads_width)

    qkv_own = project(wqkv_own, bias_own)
    mixed_own, lse_own = attend(info, qkv_own)
    qkv_oth = project(wqkv_oth, bias_oth)
    mixed_oth, lse_oth = attend(info, qkv_oth)
    mixed_own = mixed_own.reshape(total, heads_width)
    mixed_oth = mixed_oth.reshape(total, heads_width)
    residual = x + mm(mixed_own, w_out) + mm(mixed_oth, wout_oth) + b_out
    unit_mid, inv_mid = norm(residual)
    normed_mid = (unit_mid * ln2_gain + ln2_shift).astype(BF16)
    normed_mid_t = normed_mid.T
    bup_own = bias_own[2 * heads_width :][None]
    bup_oth = bias_oth[2 * heads_width :][None]
    y, gnm, gup_own, gdown_own, gbup_own = ffn(normed_mid, normed_mid_t, up, w_up, w_down, bup_own)
    y, gnm, gup_oth, gdown_oth, gbup_oth = ffn(
        normed_mid, normed_mid_t, up, wup_oth, wdown_oth, bup_oth, (y, gnm)
    )
    up_piece = reduce_pieces(gup_own, gup_oth)
    down_piece = reduce_pieces(gdown_own, gdown_oth)
    up_sum, down_sum = lax.psum((up_piece, down_piece), ("rest", "nbr"))

    out = (residual + y + b_down).astype(BF16).reshape(rows, seq, width)
    up32 = up.astype(F32)
    gl2_gain = jnp.sum(gnm * unit_mid, axis=0)
    gl2_shift = jnp.sum(gnm, axis=0)
    grad_res = up32 + norm_back(gnm, unit_mid, inv_mid, ln2_gain)
    grad_res_low = grad_res.astype(BF16)
    gm_own = mm(grad_res_low, w_out, NT).astype(BF16).reshape(rows, seq, heads_width)
    gm_oth = mm(grad_res_low, wout_oth, NT).astype(BF16).reshape(rows, seq, heads_width)
    d_oth = attend_back(info, qkv_oth, gm_oth, lse_oth).reshape(total, 3 * heads_width)
    d_own = attend_back(info, qkv_own, gm_own, lse_own).reshape(total, 3 * heads_width)
    gwout_own = mm(mixed_own, grad_res_low, TN).astype(BF16)
    gwout_oth = mm(mixed_oth, grad_res_low, TN).astype(BF16)
    gqkv_oth = mm(normed_in, d_oth, TN).astype(BF16)
    gqkv_own = mm(normed_in, d_own, TN).astype(BF16)
    qkv_piece = reduce_pieces(gqkv_own, gqkv_oth)
    wout_piece = reduce_pieces(gwout_own, gwout_oth)
    gate = lax.optimization_barrier((qkv_piece, wout_piece, up_sum, down_sum))
    qkv_piece, wout_piece, up_sum, down_sum = gate
    qkv_sum, wout_sum = lax.psum((qkv_piece, wout_piece), ("rest", "nbr"))
    grad_in = mm(d_own, wqkv_own, NT) + mm(d_oth, wqkv_oth, NT)
    gl1_gain = jnp.sum(grad_in * unit_in, axis=0)
    gl1_shift = jnp.sum(grad_in, axis=0)
    dx = (grad_res + norm_back(grad_in, unit_in, inv_in, ln1_gain)).reshape(rows, seq, width)

    def give_rows(value, sent):
        mine, got = value[:, :half], swap(sent[:, half:], "mp").astype(value.dtype)
        return join(side, mine, got)

    block_out = give_rows(out, out)
    input_grad = give_rows(dx, dx.astype(BF16))

    def bias_sums(d, gbup):
        sums = jnp.sum(d.astype(F32), axis=0)
        return [sums[:heads_width], sums[2 * heads_width :], gbup[0]]

    shared = [gl1_gain, gl1_shift, gl2_gain, gl2_shift, jnp.sum(grad_res, axis=0), jnp.sum(up32, axis=0)]
    mine = jnp.concatenate(shared + bias_sums(d_own, gbup_own))
    sent = jnp.concatenate(shared + bias_sums(d_oth, gbup_oth))
    vec = mine + swap(sent, "mp")
    vec = vec + swap(vec, "core")
    vec = vec + swap(vec, "nbr")
    step = 1
    while step < sizes["rest"]:
        vec = vec + lax.ppermute(vec, "rest", [(i, i ^ step) for i in range(sizes["rest"])])
        step *= 2
    common = [vec[i * width : (i + 1) * width] for i in range(6)]
    split = vec[6 * width :]
    qkv_grad = spread_pieces(qkv_sum)
    return (
        block_out,
        input_grad,
        common[0],
        common[1],
        qkv_grad[:, :heads_width],
        split[:heads_width],
        qkv_grad[:, heads_width : 2 * heads_width],
        qkv_grad[:, 2 * heads_width :],
        split[heads_width : 2 * heads_width],
        spread_pieces(wout_sum),
        common[4],
        common[2],
        common[3],
        spread_pieces(up_sum),
        split[2 * heads_width :],
        spread_pieces(down_sum),
        common[5],
    )


def solution(mesh):
    n_dp, n_mp = mesh.shape["dp"], mesh.shape["mp"]
    names = ("rest", "nbr", "core", "mp")
    inner = Mesh(mesh.devices.reshape(n_dp // 4, 2, 2, n_mp), names)
    dp = ("rest", "nbr", "core")
    in_specs = (
        P(dp, "mp", None),
        P(dp),
        P(dp, "mp", None),
        P(),
        P(),
        P(None, "mp"),
        P("mp"),
        P(None, "mp"),
        P(None, "mp"),
        P("mp"),
        P("mp", None),
        P(),
        P(),
        P(),
        P(None, "mp"),
        P("mp"),
        P("mp", None),
        P(),
    )
    out_specs = (
        P(dp, "mp", None),
        P(dp, "mp", None),
        P(),
        P(),
        P(None, "mp"),
        P("mp"),
        P(None, "mp"),
        P(None, "mp"),
        P("mp"),
        P("mp", None),
        P(),
        P(),
        P(),
        P(None, "mp"),
        P("mp"),
        P("mp", None),
        P(),
    )
    return jax.shard_map(
        functools.partial(on_device, dict(inner.shape)),
        mesh=inner,
        in_specs=in_specs,
        out_specs=out_specs,
        check_vma=False,
    )
```

time: 940 us -> 554 us (0.59)
  blocking collectives: 306 us -> 0 us
  matrix products: 229 us -> 22.8 us
  Pallas kernels: 0 us -> 90.3 us
  waiting for transfers between devices: 254 us -> 300 us
  other arithmetic: 87.3 us -> 58.3 us
  starting transfers between devices: 1.46 us -> 22.6 us
    all_gather x16 -> x0, blocking collectives: 206 us -> none  [the longest x4 61.2 us: on_device(): grad_full = lax.all_gather(upstream, 'mp', axis=1, tiled=True)]
    dot_general x96 -> x12, matrix products: 229 us -> 22.8 us  [mm(): return lax.dot_general(a, b, dims, preferred_element_type=F32)]
    ppermute x0 -> x34, waiting for transfers between devices: none -> 167 us  [the longest x32 160 us: swap(): return lax.ppermute(value, axis, [(0, 1), (1, 0)])]
    reduce_scatter x16 -> x0, waiting for transfers between devices: 102 us -> none  [the longest x4 50.5 us: on_device(): lax.psum_scatter(product('bsf,fd->bsd', active, w_down).astype(jnp.bfloat...]
    psum x2 -> x0, blocking collectives: 99.8 us -> none  [the longest x1 60.4 us: on_device(): lax.psum((sum_w_query, sum_b_query, sum_w_key, sum_w_value, sum_b_value,...]
    pallas_call x0 -> x6, Pallas kernels: none -> 90.3 us  [the longest x2 45.7 us: ffn(): pl.pallas_call(functools.partial(ffn_kernel, first), out_shape=(jax.Shape...]
    reduce_sum x19 -> x8, other arithmetic: 37.8 us -> 8.63 us  [the longest x1 3.11 us: on_device(): gl2_gain = jnp.sum(gnm * unit_mid, axis=0)]
    ppermute x0 -> x34, starting transfers between devices: none -> 22.5 us  [the longest x32 20.5 us: swap(): return lax.ppermute(value, axis, [(0, 1), (1, 0)])]
  transfers between devices with their start and end apart: 17 -> 36, of which waited for: 8 -> 11; matrix products, arithmetic and copies ran while one was open for 23% -> 20% of each run, Pallas kernels for 0% -> 16%
where the time goes in v1:
time: 554 us; the launch traced here: 549 us
  waiting for transfers between devices  300 us (54%)
  Pallas kernels  90.3 us (16%)
  other arithmetic  58.3 us (11%)
  local copies, waits for them, and re-layouts  39.6 us (7%)
  matrix products  22.8 us (4%)
  starting transfers between devices  22.6 us (4%)
  between operations  15.2 us (3%)
    ppermute x32, waiting for transfers between devices, swap(): return lax.ppermute(value, axis, [(0, 1), (1, 0)])  160 us
    psum x1, waiting for transfers between devices, on_device(): up_sum, down_sum = lax.psum((up_piece, down_piece), ('rest', 'nbr'))  73 us
    psum x1, waiting for transfers between devices, on_device(): qkv_sum, wout_sum = lax.psum((qkv_piece, wout_piece), ('rest', 'nbr'))  59.5 us
    pallas_call x2, Pallas kernels, ffn(): pl.pallas_call(functools.partial(ffn_kernel, first), out_shape=(jax.Shape...  45.7 us
    pallas_call x2, Pallas kernels, attend_back(): pl.pallas_call(attend_back_kernel, out_shape=jax.ShapeDtypeStruct((rows,...  25.8 us
    dot_general x12, matrix products, mm(): return lax.dot_general(a, b, dims, preferred_element_type=F32)  22.8 us
    ppermute x32, starting transfers between devices, swap(): return lax.ppermute(value, axis, [(0, 1), (1, 0)])  20.5 us
    dynamic_slice x15, local copies, waits for them, and re-layouts, part(): return lax.dynamic_slice_in_dim(value, index * size, size, 0)  19.3 us
  transfers between devices with their start and end apart: 36, of which 11 were waited for; matrix products, arithmetic and copies ran while one was open for 20% of the time, Pallas kernels for 16%

profile of v1, /device:TPU:0, one launch (start us, length us, event | category | flops | bytes accessed | tf_op | source)
XLA Modules:
  0.0 548.5 jit_solution(14576914438397560547)
XLA Ops:
  8.0 3.0 collective-permute-start.3
  30.4 58.8 %collective-permute-done = bf16[2,256,768]{2,1,0:T(8,128)(2,1)S(1)} collective-permute-done((bf16[2,256,768]{2,1,0:T(8,128)(2,1)}, bf16[2,256,768]{2,1,0:T(8,128)(2,1)S(1)}, u32[]{:S(2)}, u32[]{:S(2)}) %collective-permute-start) | collective-permute-done | bytes 786464 | tf_op jit(solution)/shard_map/ppermute | solution.py:253
  93.3 30.4 %collective-permute-done.1 = bf16[384,1152]{1,0:T(8,128)(2,1)S(1)} collective-permute-done((bf16[384,1152]{1,0:T(8,128)(2,1)}, bf16[384,1152]{1,0:T(8,128)(2,1)S(1)}, u32[]{:S(2)}, u32[]{:S(2)}) %collective-permute-start.1) | collective-permute-done | bytes 884768 | tf_op jit(solution)/shard_map/ppermute | solution.py:253
  125.4 9.5 %attend.2 = (bf16[2,512,384]{2,1,0:T(8,128)(2,1)S(1)}, f32[2,3,2,512]{3,2,1,0:T(2,128)S(1)}) custom-call(s32[3]{0:T(128)S(1)} %pad_add_fusion.info, bf16[2,512,1152]{2,1,0:T(8,128)(2,1)S(1)} %bitcast.85, bf16[2,512,1152]{2,1,0:T(8,128)(2,1)S(1)} %bitcast.86, bf16[2,512,1152]{2,1,0:T(8,128)(2,1)S(1)} %bitcast.87), custom_call_target="tpu_custom_call" | custom-call | flops 3221225472 | bytes 4718592 | tf_op jit(solution)/shard_map/attend/pallas_call | solution.py:105
  137.4 3.7 add_convert_fusion
  141.1 9.3 %attend.3 = (bf16[2,512,384]{2,1,0:T(8,128)(2,1)S(1)}, f32[2,3,2,512]{3,2,1,0:T(2,128)S(1)}) custom-call(s32[3]{0:T(128)S(1)} %pad_add_fusion.info, bf16[2,512,1152]{2,1,0:T(8,128)(2,1)S(1)} %bitcast.91, bf16[2,512,1152]{2,1,0:T(8,128)(2,1)S(1)} %bitcast.92, bf16[2,512,1152]{2,1,0:T(8,128)(2,1)S(1)} %bitcast.93), custom_call_target="tpu_custom_call" | custom-call | flops 3221225472 | bytes 4718592 | tf_op jit(solution)/shard_map/attend/pallas_call | solution.py:105
  155.9 2.6 copy.38.refs_1_
  161.3 21.8 %ffn_first.1 = (f32[1024,768]{1,0:T(8,128)}, f32[1024,768]{1,0:T(8,128)}, bf16[768,1536]{1,0:T(8,128)(2,1)}, bf16[1536,768]{1,0:T(8,128)(2,1)}, f32[1,1536]{1,0:T(1,128)S(1)}) custom-call(bf16[1024,768]{1,0:T(8,128)(2,1)S(1)} %copy-done.4, bf16[768,1024]{1,0:T(8,128)(2,1)S(1)} %copy-done.2, bf16[1024,768]{1,0:T(8,128)(2,1)} %bitcast.101, ...), custom_call_target="tpu_custom_call" | custom-call | flops 14495514624 | bytes 33030144 | tf_op jit(solution)/shard_map/ffn_first/pallas_call | solution.py:207
  183.1 2.5 constant_dynamic-slice_fusion.3
  187.2 4.0 maximum_select_fusion.2.refs_4_
  191.2 3.8 maximum_select_fusion.1.refs_3_
  195.1 23.9 %ffn_second.1 = (f32[1024,768]{1,0:T(8,128)}, f32[1024,768]{1,0:T(8,128)}, bf16[768,1536]{1,0:T(8,128)(2,1)}, bf16[1536,768]{1,0:T(8,128)(2,1)}, f32[1,1536]{1,0:T(1,128)S(1)}) custom-call(bf16[1024,768]{1,0:T(8,128)(2,1)S(1)} %copy-done.5, bf16[768,1024]{1,0:T(8,128)(2,1)S(1)} %copy-done.3, ...), custom_call_target="tpu_custom_call", output_to_operand_aliasing={{0}: (6, {}), {1}: (7, {})} | custom-call | flops 14495514624 | bytes 33030144 | tf_op jit(solution)/shard_map/ffn_second/pallas_call | solution.py:207
  219.0 3.1 multiply_reduce_fusion
  222.2 3.1 fusion.36
  233.8 12.7 %attend_back.3 = bf16[2,512,1152]{2,1,0:T(8,128)(2,1)S(1)} custom-call(s32[3]{0:T(128)S(1)} %pad_add_fusion.info, bf16[2,512,1152]{2,1,0:T(8,128)(2,1)} %bitcast.94, bf16[2,512,1152]{2,1,0:T(8,128)(2,1)} %bitcast.95, bf16[2,512,1152]{2,1,0:T(8,128)(2,1)} %bitcast.96, bf16[2,512,384]{2,1,0:T(8,128)(2,1)S(1)} %bitcast.98, ...), custom_call_target="tpu_custom_call" | custom-call | flops 8053063680 | bytes 7077888 | tf_op jit(solution)/shard_map/attend_back/pallas_call | solution.py:134
  246.9 13.1 %attend_back.2 = bf16[2,512,1152]{2,1,0:T(8,128)(2,1)S(1)} custom-call(s32[3]{0:T(128)S(1)} %pad_add_fusion.info, bf16[2,512,1152]{2,1,0:T(8,128)(2,1)} %bitcast.88, bf16[2,512,1152]{2,1,0:T(8,128)(2,1)} %bitcast.89, bf16[2,512,1152]{2,1,0:T(8,128)(2,1)} %bitcast.90, bf16[2,512,384]{2,1,0:T(8,128)(2,1)S(1)} %bitcast.97, ...), custom_call_target="tpu_custom_call" | custom-call | flops 8053063680 | bytes 7077888 | tf_op jit(solution)/shard_map/attend_back/pallas_call | solution.py:134
  263.7 3.1 fusion.19
  282.9 2.5 fusion.18
  285.5 20.8 %collective-permute-done.29 = bf16[768,768]{1,0:T(8,128)(2,1)S(1)} collective-permute-done((bf16[768,768]{1,0:T(8,128)(2,1)S(1)}, bf16[768,768]{1,0:T(8,128)(2,1)S(1)}, u32[]{:S(2)}, u32[]{:S(2)}) %collective-permute-start.29) | collective-permute-done | bytes 1179680 | tf_op jit(solution)/shard_map/ppermute | solution.py:253
  306.3 2.7 add_convert_fusion.4
  309.5 21.6 %collective-permute-done.26 = bf16[384,1536]{1,0:T(8,128)(2,1)S(1)} collective-permute-done((bf16[384,1536]{1,0:T(8,128)(2,1)S(1)}, bf16[384,1536]{1,0:T(8,128)(2,1)S(1)}, u32[]{:S(2)}, u32[]{:S(2)}) %collective-permute-start.26) | collective-permute-done | bytes 1179680 | tf_op jit(solution)/shard_map/ppermute | solution.py:253
  331.1 2.7 add_convert_fusion.6
  333.9 2.6 add_convert_fusion.9
  341.3 24.1 %collective-permute-done.23 = bf16[192,768]{1,0:T(8,128)(2,1)S(1)} collective-permute-done((bf16[192,768]{1,0:T(8,128)(2,1)S(1)}, bf16[192,768]{1,0:T(8,128)(2,1)S(1)}, u32[]{:S(2)}, u32[]{:S(2)}) %collective-permute-start.23) | collective-permute-done | bytes 294944 | tf_op jit(solution)/shard_map/ppermute | solution.py:253
  368.1 2.7 add_convert_fusion.8
  370.8 73.0 %all-reduce.7.cloned.1.call-done = (bf16[384,1536]{1,0:T(8,128)(2,1)}, bf16[768,768]{1,0:T(8,128)(2,1)}) async-done(((bf16[384,1536]{1,0:T(8,128)(2,1)}, bf16[768,768]{1,0:T(8,128)(2,1)}), (bf16[384,1536]{1,0:T(8,128)(2,1)}, bf16[768,768]{1,0:T(8,128)(2,1)})) %all-reduce.7.cloned.1.call-update) | async-done | bytes 2359312 | tf_op jit(solution)/shard_map/psum | solution.py:354
  451.0 3.3 collective-permute-done.16
  457.2 3.7 collective-permute-done.17
  464.0 2.9 maximum_select_fusion.7
  468.9 59.5 %all-reduce.5.cloned.1.call-done = (bf16[384,1152]{1,0:T(8,128)(2,1)}, bf16[192,768]{1,0:T(8,128)(2,1)}) async-done(((bf16[384,1152]{1,0:T(8,128)(2,1)}, bf16[192,768]{1,0:T(8,128)(2,1)}), (bf16[384,1152]{1,0:T(8,128)(2,1)}, bf16[192,768]{1,0:T(8,128)(2,1)})) %all-reduce.5.cloned.1.call-update) | async-done | bytes 1179664 | tf_op jit(solution)/shard_map/psum | solution.py:374
  528.9 4.3 fusion.23
  533.2 4.6 fusion.22
  (260 shorter events, 94.1 us)
Async XLA Ops:
  7.2 436.6 %all-reduce.7.cloned.1.call-start = ((), (), s32[]{:S(2)}) async-start(), calls=%async_computation.1 | async-start | bytes 4718592 | tf_op jit(solution)/shard_map/psum | solution.py:354
  8.0 20.2 %collective-permute-start.3 = (f32[2304]{0:T(1024)S(1)}, f32[2304]{0:T(1024)S(1)}, u32[]{:S(2)}, u32[]{:S(2)}) collective-permute-start(f32[2304]{0:T(1024)S(1)} %pad_maximum_fusion.2), channel_id=1, source_target_pairs={{0,1},{1,0},{2,3},{3,2},{4,5},{5,4},{6,7},{7,6},{8,9},{9,8},{10,11... | collective-permute-start | bytes 27656 | tf_op jit(solution)/shard_map/ppermute | solution.py:253
  11.7 16.9 %collective-permute-start.4 = (bf16[192,768]{1,0:T(8,128)(2,1)}, bf16[192,768]{1,0:T(8,128)(2,1)S(1)}, u32[]{:S(2)}, u32[]{:S(2)}) collective-permute-start(bf16[192,768]{1,0:T(8,128)(2,1)} %constant_dynamic-slice_fusion.12), channel_id=1, source_target_pairs={{0,1},{1,0},{2,3},{3,2},{4,5},{5,4},{6,7},{7,6},{8,9},{9,8},{10,11... | collective-permute-start | bytes 884744 | tf_op jit(solution)/shard_map/ppermute | solution.py:253
  14.5 121.4 %collective-permute-start.9 = (bf16[768,768]{1,0:T(8,128)(2,1)}, bf16[768,768]{1,0:T(8,128)(2,1)}, u32[]{:S(2)}, u32[]{:S(2)}) collective-permute-start(bf16[768,768]{1,0:T(8,128)(2,1)} %constant_dynamic-slice_fusion.8), channel_id=1, source_target_pairs={{0,1},{1,0},{2,3},{3,2},{4,5},{5,4},{6,7},{7,6},{8,9},{9,8},{10,11... | collective-permute-start | bytes 3538952 | tf_op jit(solution)/shard_map/ppermute | solution.py:253
  18.6 117.8 %collective-permute-start.7 = (bf16[384,1536]{1,0:T(8,128)(2,1)}, bf16[384,1536]{1,0:T(8,128)(2,1)}, u32[]{:S(2)}, u32[]{:S(2)}) collective-permute-start(bf16[384,1536]{1,0:T(8,128)(2,1)} %constant_dynamic-slice_fusion.9), channel_id=1, source_target_pairs={{0,1},{1,0},{2,3},{3,2},{4,5},{5,4},{6,7},{7,6},{8,9},{9,8},{10,11... | collective-permute-start | bytes 3538952 | tf_op jit(solution)/shard_map/ppermute | solution.py:253
  19.9 69.4 %collective-permute-start = (bf16[2,256,768]{2,1,0:T(8,128)(2,1)}, bf16[2,256,768]{2,1,0:T(8,128)(2,1)S(1)}, u32[]{:S(2)}, u32[]{:S(2)}) collective-permute-start(bf16[2,256,768]{2,1,0:T(8,128)(2,1)} %get-tuple-element.76), channel_id=1, source_target_pairs={{0,1},{1,0},{2,3},{3,2},{4,5},{5,4},{6,7},{7,6},{8,9},{9,8},{10,11... | collective-permute-start | bytes 2359304 | tf_op jit(solution)/shard_map/ppermute | solution.py:253
  28.2 95.4 %collective-permute-start.6 = (bf16[2,256,768]{2,1,0:T(8,128)(2,1)}, bf16[2,256,768]{2,1,0:T(8,128)(2,1)S(1)}, u32[]{:S(2)}, u32[]{:S(2)}) collective-permute-start(bf16[2,256,768]{2,1,0:T(8,128)(2,1)} %get-tuple-element.74), channel_id=1, source_target_pairs={{0,1},{1,0},{2,3},{3,2},{4,5},{5,4},{6,7},{7,6},{8,9},{9,8},{10,11... | collective-permute-start | bytes 2359304 | tf_op jit(solution)/shard_map/ppermute | solution.py:253
  28.6 95.0 %collective-permute-start.1 = (bf16[384,1152]{1,0:T(8,128)(2,1)}, bf16[384,1152]{1,0:T(8,128)(2,1)S(1)}, u32[]{:S(2)}, u32[]{:S(2)}) collective-permute-start(bf16[384,1152]{1,0:T(8,128)(2,1)} %constant_dynamic-slice_fusion.13), channel_id=1, source_target_pairs={{0,1},{1,0},{2,3},{3,2},{4,5},{5,4},{6,7},{7,6},{8,9},{9,8},{10,11... | collective-permute-start | bytes 2654216 | tf_op jit(solution)/shard_map/ppermute | solution.py:253
  89.3 61.2 %collective-permute-start.5 = (bf16[192,768]{1,0:T(8,128)(2,1)S(1)}, bf16[192,768]{1,0:T(8,128)(2,1)S(1)}, u32[]{:S(2)}, u32[]{:S(2)}) collective-permute-start(bf16[192,768]{1,0:T(8,128)(2,1)S(1)} %collective-permute-done.4), channel_id=1, source_target_pairs={{0,2},{2,0},{1,3},{3,1},{4,6},{6,4},{5,7},{7,5},{8,10},{10,8},{9,1... | collective-permute-start | bytes 884744 | tf_op jit(solution)/shard_map/ppermute | solution.py:253
  123.6 12.9 %collective-permute-start.2 = (bf16[384,1152]{1,0:T(8,128)(2,1)S(1)}, bf16[384,1152]{1,0:T(8,128)(2,1)S(1)}, u32[]{:S(2)}, u32[]{:S(2)}) collective-permute-start(bf16[384,1152]{1,0:T(8,128)(2,1)S(1)} %collective-permute-done.1), channel_id=1, source_target_pairs={{0,2},{2,0},{1,3},{3,1},{4,6},{6,4},{5,7},{7,5},{8,10},{10,8},{9,1... | collective-permute-start | bytes 2654216 | tf_op jit(solution)/shard_map/ppermute | solution.py:253
  135.9 51.3 %collective-permute-start.10 = (bf16[768,768]{1,0:T(8,128)(2,1)}, bf16[768,768]{1,0:T(8,128)(2,1)}, u32[]{:S(2)}, u32[]{:S(2)}) collective-permute-start(bf16[768,768]{1,0:T(8,128)(2,1)} %collective-permute-done.9), channel_id=1, source_target_pairs={{0,2},{2,0},{1,3},{3,1},{4,6},{6,4},{5,7},{7,5},{8,10},{10,8},{9,1... | collective-permute-start | bytes 3538952 | tf_op jit(solution)/shard_map/ppermute | solution.py:253
  136.4 54.8 %collective-permute-start.8 = (bf16[384,1536]{1,0:T(8,128)(2,1)}, bf16[384,1536]{1,0:T(8,128)(2,1)}, u32[]{:S(2)}, u32[]{:S(2)}) collective-permute-start(bf16[384,1536]{1,0:T(8,128)(2,1)} %collective-permute-done.7), channel_id=1, source_target_pairs={{0,2},{2,0},{1,3},{3,1},{4,6},{6,4},{5,7},{7,5},{8,10},{10,8},{9,1... | collective-permute-start | bytes 3538952 | tf_op jit(solution)/shard_map/ppermute | solution.py:253
  185.6 123.4 %collective-permute-start.24 = (bf16[384,1536]{1,0:T(8,128)(2,1)}, bf16[384,1536]{1,0:T(8,128)(2,1)}, u32[]{:S(2)}, u32[]{:S(2)}) collective-permute-start(bf16[384,1536]{1,0:T(8,128)(2,1)} %constant_dynamic-slice_fusion.3), channel_id=1, source_target_pairs={{0,2},{2,0},{1,3},{3,1},{4,6},{6,4},{5,7},{7,5},{8,10},{10,8},{9,1... | collective-permute-start | bytes 3538952 | tf_op jit(solution)/shard_map/ppermute | solution.py:253
  187.1 98.4 %collective-permute-start.27 = (bf16[768,768]{1,0:T(8,128)(2,1)}, bf16[768,768]{1,0:T(8,128)(2,1)}, u32[]{:S(2)}, u32[]{:S(2)}) collective-permute-start(bf16[768,768]{1,0:T(8,128)(2,1)} %constant_dynamic-slice_fusion.1), channel_id=1, source_target_pairs={{0,2},{2,0},{1,3},{3,1},{4,6},{6,4},{5,7},{7,5},{8,10},{10,8},{9,1... | collective-permute-start | bytes 3538952 | tf_op jit(solution)/shard_map/ppermute | solution.py:253
  229.2 234.8 %collective-permute-start.11 = (bf16[2,256,768]{2,1,0:T(8,128)(2,1)}, bf16[2,256,768]{2,1,0:T(8,128)(2,1)}, u32[]{:S(2)}, u32[]{:S(2)}) collective-permute-start(bf16[2,256,768]{2,1,0:T(8,128)(2,1)} %get-tuple-element.72), channel_id=1, source_target_pairs={{0,1},{1,0},{2,3},{3,2},{4,5},{5,4},{6,7},{7,6},{8,9},{9,8},{10,11... | collective-permute-start | bytes 2359304 | tf_op jit(solution)/shard_map/ppermute | solution.py:253
  232.3 43.0 %collective-permute-start.28 = (bf16[768,768]{1,0:T(8,128)(2,1)}, bf16[768,768]{1,0:T(8,128)(2,1)}, u32[]{:S(2)}, u32[]{:S(2)}) collective-permute-start(bf16[768,768]{1,0:T(8,128)(2,1)} %constant_dynamic-slice_fusion), channel_id=1, source_target_pairs={{0,2},{2,0},{1,3},{3,1},{4,6},{6,4},{5,7},{7,5},{8,10},{10,8},{9,1... | collective-permute-start | bytes 3538952 | tf_op jit(solution)/shard_map/ppermute | solution.py:253
  232.7 45.9 %collective-permute-start.25 = (bf16[384,1536]{1,0:T(8,128)(2,1)}, bf16[384,1536]{1,0:T(8,128)(2,1)}, u32[]{:S(2)}, u32[]{:S(2)}) collective-permute-start(bf16[384,1536]{1,0:T(8,128)(2,1)} %constant_dynamic-slice_fusion.2), channel_id=1, source_target_pairs={{0,2},{2,0},{1,3},{3,1},{4,6},{6,4},{5,7},{7,5},{8,10},{10,8},{9,1... | collective-permute-start | bytes 3538952 | tf_op jit(solution)/shard_map/ppermute | solution.py:253
  277.5 28.8 %collective-permute-start.29 = (bf16[768,768]{1,0:T(8,128)(2,1)S(1)}, bf16[768,768]{1,0:T(8,128)(2,1)S(1)}, u32[]{:S(2)}, u32[]{:S(2)}) collective-permute-start(bf16[768,768]{1,0:T(8,128)(2,1)S(1)} %add_convert_fusion.5), channel_id=1, source_target_pairs={{0,1},{1,0},{2,3},{3,2},{4,5},{5,4},{6,7},{7,6},{8,9},{9,8},{10,11... | collective-permute-start | bytes 3538952 | tf_op jit(solution)/shard_map/ppermute | solution.py:253
  280.2 51.0 %collective-permute-start.26 = (bf16[384,1536]{1,0:T(8,128)(2,1)S(1)}, bf16[384,1536]{1,0:T(8,128)(2,1)S(1)}, u32[]{:S(2)}, u32[]{:S(2)}) collective-permute-start(bf16[384,1536]{1,0:T(8,128)(2,1)S(1)} %add_convert_fusion.7), channel_id=1, source_target_pairs={{0,1},{1,0},{2,3},{3,2},{4,5},{5,4},{6,7},{7,6},{8,9},{9,8},{10,11... | collective-permute-start | bytes 3538952 | tf_op jit(solution)/shard_map/ppermute | solution.py:253
  285.5 53.6 %collective-permute-start.22 = (bf16[192,768]{1,0:T(8,128)(2,1)}, bf16[192,768]{1,0:T(8,128)(2,1)S(1)}, u32[]{:S(2)}, u32[]{:S(2)}) collective-permute-start(bf16[192,768]{1,0:T(8,128)(2,1)} %constant_dynamic-slice_fusion.4), channel_id=1, source_target_pairs={{0,2},{2,0},{1,3},{3,1},{4,6},{6,4},{5,7},{7,5},{8,10},{10,8},{9,1... | collective-permute-start | bytes 884744 | tf_op jit(solution)/shard_map/ppermute | solution.py:253
  306.3 27.6 %collective-permute-start.19 = (bf16[384,1152]{1,0:T(8,128)(2,1)}, bf16[384,1152]{1,0:T(8,128)(2,1)}, u32[]{:S(2)}, u32[]{:S(2)}) collective-permute-start(bf16[384,1152]{1,0:T(8,128)(2,1)} %constant_dynamic-slice_fusion.6), channel_id=1, source_target_pairs={{0,2},{2,0},{1,3},{3,1},{4,6},{6,4},{5,7},{7,5},{8,10},{10,8},{9,1... | collective-permute-start | bytes 2654216 | tf_op jit(solution)/shard_map/ppermute | solution.py:253
  309.0 31.4 %collective-permute-start.21 = (bf16[192,768]{1,0:T(8,128)(2,1)}, bf16[192,768]{1,0:T(8,128)(2,1)}, u32[]{:S(2)}, u32[]{:S(2)}) collective-permute-start(bf16[192,768]{1,0:T(8,128)(2,1)} %constant_dynamic-slice_fusion.5), channel_id=1, source_target_pairs={{0,2},{2,0},{1,3},{3,1},{4,6},{6,4},{5,7},{7,5},{8,10},{10,8},{9,1... | collective-permute-start | bytes 884744 | tf_op jit(solution)/shard_map/ppermute | solution.py:253
  331.1 36.9 %collective-permute-start.18 = (bf16[384,1152]{1,0:T(8,128)(2,1)}, bf16[384,1152]{1,0:T(8,128)(2,1)}, u32[]{:S(2)}, u32[]{:S(2)}) collective-permute-start(bf16[384,1152]{1,0:T(8,128)(2,1)} %constant_dynamic-slice_fusion.7), channel_id=1, source_target_pairs={{0,2},{2,0},{1,3},{3,1},{4,6},{6,4},{5,7},{7,5},{8,10},{10,8},{9,1... | collective-permute-start | bytes 2654216 | tf_op jit(solution)/shard_map/ppermute | solution.py:253
  333.9 194.5 %all-reduce.5.cloned.1.call-start = ((), (), s32[]{:S(2)}) async-start(), calls=%async_computation | async-start | bytes 2359296 | tf_op jit(solution)/shard_map/psum | solution.py:374
  336.6 31.5 %collective-permute-start.20 = (bf16[384,1152]{1,0:T(8,128)(2,1)}, bf16[384,1152]{1,0:T(8,128)(2,1)}, u32[]{:S(2)}, u32[]{:S(2)}) collective-permute-start(bf16[384,1152]{1,0:T(8,128)(2,1)} %add_convert_fusion.9), channel_id=1, source_target_pairs={{0,1},{1,0},{2,3},{3,2},{4,5},{5,4},{6,7},{7,6},{8,9},{9,8},{10,11... | collective-permute-start | bytes 2654216 | tf_op jit(solution)/shard_map/ppermute | solution.py:253
  339.1 26.3 %collective-permute-start.23 = (bf16[192,768]{1,0:T(8,128)(2,1)S(1)}, bf16[192,768]{1,0:T(8,128)(2,1)S(1)}, u32[]{:S(2)}, u32[]{:S(2)}) collective-permute-start(bf16[192,768]{1,0:T(8,128)(2,1)S(1)} %add_convert_fusion.11), channel_id=1, source_target_pairs={{0,1},{1,0},{2,3},{3,2},{4,5},{5,4},{6,7},{7,6},{8,9},{9,8},{10,11... | collective-permute-start | bytes 884744 | tf_op jit(solution)/shard_map/ppermute | solution.py:253
  340.4 103.4 %collective-permute-start.13 = (f32[6912]{0:T(1024)S(1)}, f32[6912]{0:T(1024)S(1)}, u32[]{:S(2)}, u32[]{:S(2)}) collective-permute-start(f32[6912]{0:T(1024)S(1)} %constant_dynamic-update-slice_fusion.8), channel_id=1, source_target_pairs={{0,1},{1,0},{2,3},{3,2},{4,5},{5,4},{6,7},{7,6},{8,9},{9,8},{10,11... | collective-permute-start | bytes 82952 | tf_op jit(solution)/shard_map/ppermute | solution.py:253
  365.5 97.3 %collective-permute-start.12 = (bf16[2,256,768]{2,1,0:T(8,128)(2,1)S(1)}, bf16[2,256,768]{2,1,0:T(8,128)(2,1)}, u32[]{:S(2)}, u32[]{:S(2)}) collective-permute-start(bf16[2,256,768]{2,1,0:T(8,128)(2,1)S(1)} %slice.124), channel_id=1, source_target_pairs={{0,1},{1,0},{2,3},{3,2},{4,5},{5,4},{6,7},{7,6},{8,9},{9,8},{10,11... | collective-permute-start | bytes 2359304 | tf_op jit(solution)/shard_map/ppermute | solution.py:253
  443.8 85.1 %collective-permute-start.33 = (bf16[768,768]{1,0:T(8,128)(2,1)}, bf16[768,768]{1,0:T(8,128)(2,1)}, u32[]{:S(2)}, u32[]{:S(2)}) collective-permute-start(bf16[768,768]{1,0:T(8,128)(2,1)} %get-tuple-element.52), channel_id=1, source_target_pairs={{0,2},{2,0},{1,3},{3,1},{4,6},{6,4},{5,7},{7,5},{8,10},{10,8},{9,1... | collective-permute-start | bytes 3538952 | tf_op jit(solution)/shard_map/ppermute | solution.py:253
  461.5 71.7 %collective-permute-start.32 = (bf16[384,1536]{1,0:T(8,128)(2,1)S(1)}, bf16[384,1536]{1,0:T(8,128)(2,1)}, u32[]{:S(2)}, u32[]{:S(2)}) collective-permute-start(bf16[384,1536]{1,0:T(8,128)(2,1)S(1)} %copy-done.31), channel_id=1, source_target_pairs={{0,2},{2,0},{1,3},{3,1},{4,6},{6,4},{5,7},{7,5},{8,10},{10,8},{9,1... | collective-permute-start | bytes 3538952 | tf_op jit(solution)/shard_map/ppermute | solution.py:253
  528.4 9.4 %collective-permute-start.31 = (bf16[192,768]{1,0:T(8,128)(2,1)}, bf16[192,768]{1,0:T(8,128)(2,1)S(1)}, u32[]{:S(2)}, u32[]{:S(2)}) collective-permute-start(bf16[192,768]{1,0:T(8,128)(2,1)} %get-tuple-element.62), channel_id=1, source_target_pairs={{0,2},{2,0},{1,3},{3,1},{4,6},{6,4},{5,7},{7,5},{8,10},{10,8},{9,1... | collective-permute-start | bytes 884744 | tf_op jit(solution)/shard_map/ppermute | solution.py:253
  528.4 10.5 %collective-permute-start.30 = (bf16[384,1152]{1,0:T(8,128)(2,1)}, bf16[384,1152]{1,0:T(8,128)(2,1)S(1)}, u32[]{:S(2)}, u32[]{:S(2)}) collective-permute-start(bf16[384,1152]{1,0:T(8,128)(2,1)} %get-tuple-element.61), channel_id=1, source_target_pairs={{0,2},{2,0},{1,3},{3,1},{4,6},{6,4},{5,7},{7,5},{8,10},{10,8},{9,1... | collective-permute-start | bytes 2654216 | tf_op jit(solution)/shard_map/ppermute | solution.py:253
  (56 other events, 596.2 us)
Sparse Core Ops, SparseCore 0:
  334.0 109.7 all-reduce.6
  448.3 80.0 all-reduce.4

commit v2 on v1

v2 whole, which is shorter than its diff:
```python
import functools
import math

import jax
import jax.numpy as jnp
from jax import lax
from jax.experimental import pallas as pl
from jax.experimental.pallas import tpu as pltpu
from jax.sharding import Mesh
from jax.sharding import PartitionSpec as P

HEAD_DIM = 64
PAIR = 2 * HEAD_DIM
EPS = 1e-12
FILL = -1000000000.0
SCALE = 1.0 / math.sqrt(HEAD_DIM)
LOG2E = math.log2(math.e)
F32 = jnp.float32
BF16 = jnp.bfloat16
NT = (((1,), (1,)), ((), ()))
NN = (((1,), (0,)), ((), ()))
TN = (((0,), (0,)), ((), ()))


def mm(a, b, dims=NN):
    return lax.dot_general(a, b, dims, preferred_element_type=F32)


def key_mask(info, row, shape):
    seq = shape[0]
    slot = lax.broadcasted_iota(jnp.int32, shape, 0) + info[0]
    position = jnp.where(slot >= seq, slot - seq, slot)
    return position < info[1 + row]


def head_lanes(value, head):
    lane = lax.broadcasted_iota(jnp.int32, value.shape, 1)
    keep = lane < HEAD_DIM if head == 0 else lane >= HEAD_DIM
    return jnp.where(keep, value, jnp.zeros_like(value))


def attend_kernel(info, q_ref, k_ref, v_ref, o_ref, lse_ref):
    row = pl.program_id(0)
    q, k, v = q_ref[0], k_ref[0], v_ref[0]
    valid = key_mask(info, row, (k.shape[0], q.shape[0]))
    v_t = v.T
    parts = []
    for head in range(2):
        scores = mm(head_lanes(k, head), q, NT) * (SCALE * LOG2E)
        scores = jnp.where(valid, scores, FILL * LOG2E)
        top = jnp.max(scores, axis=0, keepdims=True)
        weight = jnp.exp2(scores - top)
        total = jnp.sum(weight, axis=0, keepdims=True)
        lse_ref[0, 0, head : head + 1, :] = top + jnp.log2(total)
        probs = (weight * (1.0 / total)).astype(BF16)
        parts.append(mm(v_t[head * HEAD_DIM : (head + 1) * HEAD_DIM], probs))
    o_ref[0] = jnp.concatenate(parts, axis=0).T.astype(BF16)


def attend_back_kernel(info, q_ref, k_ref, v_ref, do_ref, lse_ref, d_ref):
    row = pl.program_id(0)
    pair = pl.program_id(1)
    n_pairs = pl.num_programs(1)
    q, k, v, do = q_ref[0], k_ref[0], v_ref[0], do_ref[0]
    valid = key_mask(info, row, (k.shape[0], q.shape[0]))
    k_t = k.T
    dq_t, dk, dv = [], [], []
    for head in range(2):
        scores = mm(head_lanes(k, head), q, NT) * (SCALE * LOG2E)
        scores = jnp.where(valid, scores, FILL * LOG2E)
        probs = jnp.exp2(scores - lse_ref[0, 0, head : head + 1, :])
        dv.append(mm(probs.astype(BF16), do))
        dprobs = mm(head_lanes(v, head), do, NT)
        delta = jnp.sum(probs * dprobs, axis=0, keepdims=True)
        dscores = (probs * (dprobs - delta)).astype(BF16)
        dk.append(mm(dscores, q))
        dq_t.append(mm(k_t[head * HEAD_DIM : (head + 1) * HEAD_DIM], dscores))
    first = lax.broadcasted_iota(jnp.int32, dv[0].shape, 1) < HEAD_DIM
    dq = jnp.concatenate(dq_t, axis=0).T * SCALE

    def put(slot, value):
        start = pl.multiple_of((slot * n_pairs + pair) * PAIR, PAIR)
        d_ref[0, :, pl.ds(start, PAIR)] = value.astype(BF16)

    put(0, dq)
    put(1, jnp.where(first, dk[0], dk[1]) * SCALE)
    put(2, jnp.where(first, dv[0], dv[1]))


def attend_specs(seq, n_pairs):
    return [
        pl.BlockSpec((1, seq, PAIR), lambda r, p, info: (r, 0, p)),
        pl.BlockSpec((1, seq, PAIR), lambda r, p, info: (r, 0, n_pairs + p)),
        pl.BlockSpec((1, seq, PAIR), lambda r, p, info: (r, 0, 2 * n_pairs + p)),
    ]


VMEM_LIMIT = 50 * 1024 * 1024


def cost(micros):
    return pl.CostEstimate(flops=int(micros * 1.15e9), bytes_accessed=1000, transcendentals=0)


def attend(info, qkv):
    rows, seq, width = qkv.shape
    n_pairs = width // (3 * PAIR)
    return pl.pallas_call(
        attend_kernel,
        out_shape=(
            jax.ShapeDtypeStruct((rows, seq, n_pairs * PAIR), BF16),
            jax.ShapeDtypeStruct((rows, n_pairs, 2, seq), F32),
        ),
        grid_spec=pltpu.PrefetchScalarGridSpec(
            num_scalar_prefetch=1,
            grid=(rows, n_pairs),
            in_specs=attend_specs(seq, n_pairs),
            out_specs=(
                pl.BlockSpec((1, seq, PAIR), lambda r, p, info: (r, 0, p)),
                pl.BlockSpec((1, 1, 2, seq), lambda r, p, info: (r, p, 0, 0)),
            ),
        ),
        compiler_params=pltpu.CompilerParams(vmem_limit_bytes=VMEM_LIMIT),
        cost_estimate=cost(10),
        name="attend",
    )(info, qkv, qkv, qkv)


def attend_back(info, qkv, grad_mixed, lse):
    rows, seq, width = qkv.shape
    n_pairs = width // (3 * PAIR)
    return pl.pallas_call(
        attend_back_kernel,
        out_shape=jax.ShapeDtypeStruct((rows, seq, width), BF16),
        grid_spec=pltpu.PrefetchScalarGridSpec(
            num_scalar_prefetch=1,
            grid=(rows, n_pairs),
            in_specs=attend_specs(seq, n_pairs)
            + [
                pl.BlockSpec((1, seq, PAIR), lambda r, p, info: (r, 0, p)),
                pl.BlockSpec((1, 1, 2, seq), lambda r, p, info: (r, p, 0, 0)),
            ],
            out_specs=pl.BlockSpec((1, seq, width), lambda r, p, info: (r, 0, 0)),
        ),
        compiler_params=pltpu.CompilerParams(vmem_limit_bytes=VMEM_LIMIT),
        cost_estimate=cost(13),
        name="attend_back",
    )(info, qkv, qkv, qkv, grad_mixed, lse)


def ffn_kernel(mode, block, info, *refs):
    first, own = mode
    refs = list(refs)
    nm, nm_t, up = refs[:3]
    wa, wb, bu = refs[3:6]
    y_in, gnm_in = (None, None) if first else refs[6:8]
    y, gnm, keep, send, gbu = refs[-5:]
    step = pl.program_id(0)
    core = info[0]

    @pl.when(step == 0)
    def _():
        if first:
            y[...] = jnp.zeros_like(y)
            gnm[...] = jnp.zeros_like(gnm)
        else:
            y[...] = y_in[...]
            gnm[...] = gnm_in[...]

    x, g = nm[...], up[...]
    width = x.shape[1]
    per = width // block
    start = pl.multiple_of(lax.rem(step, per) * block, block)
    part = pl.ds(start, block)
    if own:
        w_up, w_down = wa[...], wb[...]
    else:
        w_up = jnp.where(core == 0, wa[:, part], wb[:, part])
        w_down = jnp.where(core == 0, wb[part, :], wa[part, :])
    hidden = mm(x, w_up) + bu[...]
    cdf = 0.5 * (1.0 + lax.erf(hidden * (1.0 / math.sqrt(2.0))))
    active = (hidden * cdf).astype(BF16)
    slope = cdf + hidden * jnp.exp(-0.5 * hidden * hidden) * (1.0 / math.sqrt(2.0 * math.pi))
    grad_hidden = (mm(g, w_down, NT) * slope).astype(BF16)
    gbu[...] = jnp.sum(grad_hidden.astype(F32), axis=0, keepdims=True)
    y[...] += mm(active, w_down)
    gnm[...] += mm(grad_hidden, w_up, NT)
    grad_down = mm(active, g, TN).astype(BF16)
    grad_up = mm(nm_t[...], grad_hidden).astype(BF16)

    @pl.when(core == 0)
    def _():
        keep[0, :, part] = grad_up
        send[0, part, :] = grad_down

    @pl.when(core != 0)
    def _():
        keep[0, part, :] = grad_down
        send[0, :, part] = grad_up


def ffn(core, nm, nm_t, up, wa, wb, bu, own, sums=None, block=256):
    tokens, width = nm.shape
    units = bu.shape[1]
    first = sums is None
    per = width // block
    whole = lambda shape: pl.BlockSpec(shape, lambda f, info: (0, 0))
    once = lambda shape: pl.BlockSpec(shape, lambda f, info: (0, 0), pipeline_mode=pl.Buffered(1))
    in_specs = [once((tokens, width)), once((width, tokens)), once((tokens, width))]
    if own:
        in_specs += [
            pl.BlockSpec((width, block), lambda f, info: (0, f)),
            pl.BlockSpec((block, width), lambda f, info: (f, 0)),
        ]
    else:
        in_specs += [once((width, width))] * 2
    in_specs += [pl.BlockSpec((1, block), lambda f, info: (0, f))]
    args = [nm, nm_t, up, wa, wb, bu]
    aliases = {}
    if not first:
        in_specs += [once((tokens, width))] * 2
        args += list(sums)
        aliases = {7: 0, 8: 1}
    grads = pl.BlockSpec((1, width, width), lambda f, info: (f // per, 0, 0))
    return pl.pallas_call(
        functools.partial(ffn_kernel, (first, own), block),
        out_shape=(
            jax.ShapeDtypeStruct((tokens, width), F32),
            jax.ShapeDtypeStruct((tokens, width), F32),
            jax.ShapeDtypeStruct((units // width, width, width), BF16),
            jax.ShapeDtypeStruct((units // width, width, width), BF16),
            jax.ShapeDtypeStruct((1, units), F32),
        ),
        grid_spec=pltpu.PrefetchScalarGridSpec(
            num_scalar_prefetch=1,
            grid=(units // block,),
            in_specs=in_specs,
            out_specs=(
                whole((tokens, width)),
                whole((tokens, width)),
                grads,
                grads,
                pl.BlockSpec((1, block), lambda f, info: (0, f)),
            ),
        ),
        input_output_aliases=aliases,
        compiler_params=pltpu.CompilerParams(vmem_limit_bytes=VMEM_LIMIT),
        cost_estimate=cost(22 if own else 15),
        name="ffn_own" if own else "ffn_other",
    )(core, *args)


def norm(values):
    average = jnp.mean(values, axis=-1, keepdims=True)
    centred = values - average
    inv = lax.rsqrt(jnp.mean(centred * centred, axis=-1, keepdims=True) + EPS)
    return centred * inv, inv


def norm_back(grad, unit, inv, gain):
    scaled = grad * gain
    return inv * (
        scaled
        - jnp.mean(scaled, axis=-1, keepdims=True)
        - unit * jnp.mean(scaled * unit, axis=-1, keepdims=True)
    )


def swap(value, axis):
    return lax.ppermute(value, axis, [(0, 1), (1, 0)])


def part(value, index, count):
    size = value.shape[0] // count
    return lax.dynamic_slice_in_dim(value, index * size, size, 0)


def join(index, mine, other):
    return jnp.where(index == 0, jnp.concatenate([mine, other]), jnp.concatenate([other, mine]))


def tie(*values):
    return lax.optimization_barrier(values)


def add_low(a, b):
    return (a.astype(F32) + b.astype(F32)).astype(BF16)


def ladder(sizes):
    steps = [("nbr", lax.axis_index("nbr"), [(0, 1), (1, 0)])]
    bit = 1
    while bit < sizes["rest"]:
        index = (lax.axis_index("rest") // bit) % 2
        steps.append(("rest", index, [(i, i ^ bit) for i in range(sizes["rest"])]))
        bit *= 2
    return steps


def halve(value, step):
    axis, index, perm = step
    got = lax.ppermute(part(value, 1 - index, 2), axis, perm)
    return add_low(part(value, index, 2), got)


def double(value, step):
    axis, index, perm = step
    return join(index, value, lax.ppermute(value, axis, perm))


class Chain:
    def __init__(self, value, moves):
        self.value, self.moves = value, list(moves)

    def go(self):
        if self.moves:
            self.value = self.moves.pop(0)(self.value)


def meet(chains, *values):
    tied = tie(*[c.value for c in chains], *values)
    for c, v in zip(chains, tied):
        c.value = v
    rest = tied[len(chains) :]
    return rest[0] if len(rest) == 1 else rest


def on_device(
    sizes,
    tokens,
    lengths,
    out_grad,
    ln1_gain,
    ln1_shift,
    w_query,
    b_query,
    w_key,
    w_value,
    b_value,
    w_out,
    b_out,
    ln2_gain,
    ln2_shift,
    w_up,
    b_up,
    w_down,
    b_down,
):
    side = lax.axis_index("mp")
    core = lax.axis_index("core")
    nbr = lax.axis_index("nbr")
    rows_dev, half, width = tokens.shape
    rows = rows_dev // 2
    seq = 2 * half
    total = rows * seq
    heads = w_query.shape[1]
    units = w_up.shape[1] // 2
    steps = ladder(sizes)

    def by_core(first, second):
        return jnp.where(core == 0, first, second)

    def take_rows(mine, got):
        return jnp.concatenate([part(mine, side, 2), got], axis=1).reshape(total, width)

    w_send = jnp.where(
        nbr == 0, by_core(w_query, w_value), by_core(w_key, w_out.T)
    )
    w_send, t_send = tie(w_send, part(tokens, 1 - side, 2))
    w_mine = swap(w_send, "mp")
    got_tokens = swap(t_send, "mp")
    bias_own = jnp.concatenate([b_query, b_value, b_up])
    w_mine, bias_own = tie(w_mine, bias_own)
    bias_oth = swap(bias_own, "mp")
    w_near = swap(w_mine, "nbr")
    w_pair = jnp.where(
        nbr == 0, jnp.concatenate([w_mine, w_near]), jnp.concatenate([w_near, w_mine])
    )
    w_cross = swap(w_pair, "core")
    up_halves = [w_up[:, :units], w_up[:, units:]]
    down_halves = [w_down[:units], w_down[units:]]
    f_send0 = part(by_core(up_halves[0], down_halves[0]), nbr, 2)
    f_send1 = by_core(up_halves[1], down_halves[1])
    g_send = part(out_grad, 1 - side, 2)
    got_tokens, f_send0, g_send = tie(got_tokens, f_send0, g_send)
    x_low = take_rows(tokens, got_tokens)
    f_mine0 = swap(f_send0, "mp")
    x = x_low.astype(F32)
    wqkv_own = jnp.concatenate([w_query, w_key, w_value], axis=1)
    info = jnp.concatenate([(side * half)[None].astype(jnp.int32), part(lengths, side, 2)])
    q_k = by_core(w_pair, w_cross)
    v_o = by_core(w_cross, w_pair)
    wqkv_oth = jnp.concatenate([q_k[:width], q_k[width:], v_o[:width]], axis=1)
    wout_t = v_o[width:]

    unit_in, inv_in = norm(x)
    normed_in = (unit_in * ln1_gain + ln1_shift).astype(BF16)

    def project(weight, bias):
        no_key = jnp.zeros((heads,), F32)
        full = jnp.concatenate([bias[:heads], no_key, bias[heads : 2 * heads]])
        return (mm(normed_in, weight) + full).astype(BF16).reshape(rows, seq, 3 * heads)

    qkv_own = project(wqkv_own, bias_own)
    qkv_oth = project(wqkv_oth, bias_oth)
    qkv_own, qkv_oth = tie(qkv_own, qkv_oth)
    mixed_own, lse_own = attend(info, qkv_own)
    qkv_oth, f_mine0, f_send1, mixed_own = tie(qkv_oth, f_mine0, f_send1, mixed_own)
    f_mine1 = swap(f_send1, "mp")
    got_grad = swap(g_send, "mp")
    f_half0 = join(nbr, f_mine0, swap(f_mine0, "nbr"))
    mixed_oth, lse_oth = attend(info, qkv_oth)
    mixed_oth, f_half0, got_grad = tie(mixed_oth, f_half0, got_grad)
    up = take_rows(out_grad, got_grad)
    f_cross0 = swap(f_half0, "core")
    mixed_own = mixed_own.reshape(total, heads)
    mixed_oth = mixed_oth.reshape(total, heads)
    residual = x + mm(mixed_own, w_out) + mm(mixed_oth, wout_t, NT) + b_out
    unit_mid, inv_mid = norm(residual)
    normed_mid = (unit_mid * ln2_gain + ln2_shift).astype(BF16)
    normed_mid_t = normed_mid.T
    bup_own = bias_own[2 * heads :][None]
    bup_oth = bias_oth[2 * heads :][None]
    core_info = core.astype(jnp.int32)[None]
    feed = functools.partial(ffn, core_info, normed_mid, normed_mid_t, up)

    y, gnm, f_keep0, f_give0, gbup0 = feed(f_half0, f_cross0, bup_oth[:, :units], False)
    f_keep0, f_give0 = f_keep0[0], f_give0[0]
    y, f_give0, f_mine1 = tie(y, f_give0, f_mine1)
    f_cross1 = swap(f_mine1, "core")
    f_swap0 = swap(f_give0, "core")
    y, gnm, f_keep1, f_give1, gbup1 = feed(f_mine1, f_cross1, bup_oth[:, units:], False, (y, gnm))
    f_keep1, f_give1 = f_keep1[0], f_give1[0]
    y, f_oth0, f_give1 = tie(y, add_low(f_keep0, f_swap0), f_give1)
    f_got0 = swap(f_oth0, "mp")
    f_swap1 = swap(f_give1, "core")
    y, gnm, f_keep_own, f_give_own, gbup_own = feed(w_up, w_down, bup_own, True, (y, gnm))
    gnm, f_got0, f_oth1, f_give_own = tie(gnm, f_got0, add_low(f_keep1, f_swap1), f_give_own)
    f_got1 = swap(f_oth1, "mp")
    f_own = add_low(f_keep_own, swap(f_give_own, "core"))

    up32 = up.astype(F32)
    gl2_gain = jnp.sum(gnm * unit_mid, axis=0)
    gl2_shift = jnp.sum(gnm, axis=0)
    grad_res = up32 + norm_back(gnm, unit_mid, inv_mid, ln2_gain)
    grad_res_low = grad_res.astype(BF16)
    gm_own = mm(grad_res_low, w_out, NT).astype(BF16).reshape(rows, seq, heads)
    gm_oth = mm(grad_res_low, wout_t).astype(BF16).reshape(rows, seq, heads)
    moves = [functools.partial(halve, step=step) for step in steps]
    moves += [functools.partial(double, step=step) for step in reversed(steps)]
    moves += [lambda v: (v, swap(v, "core"))]
    f0 = Chain(add_low(f_own[0], f_got0), moves)
    gm_oth = meet([f0], gm_oth)
    f0.go()
    d_oth = attend_back(info, qkv_oth, gm_oth, lse_oth).reshape(total, 3 * heads)
    d_oth, f_got1 = meet([f0], d_oth, f_got1)
    f1 = Chain(add_low(f_own[1], f_got1), moves)

    def core_sum(first, second):
        return add_low(by_core(first, second), swap(by_core(second, first), "core"))

    def attn_sum(d, mixed):
        g = mm(normed_in, d, TN).astype(BF16)
        o = mm(grad_res_low, mixed, TN).astype(BF16)
        return core_sum(g[:, : 2 * heads], jnp.concatenate([g[:, 2 * heads :], o], axis=1))

    a_oth = attn_sum(d_oth, mixed_oth)
    gm_own, a_oth = meet([f0, f1], gm_own, a_oth)
    a_got = swap(a_oth, "mp")
    f0.go()
    f1.go()
    d_own = attend_back(info, qkv_own, gm_own, lse_own).reshape(total, 3 * heads)
    d_own = meet([f0, f1], d_own)
    f0.go()
    a_own = attn_sum(d_own, mixed_own)
    d_own, a_own = meet([f0], d_own, a_own)
    f0.go()
    f1.go()
    grad_in = mm(d_own, wqkv_own, NT) + mm(d_oth, wqkv_oth, NT)
    gl1_gain = jnp.sum(grad_in * unit_in, axis=0)
    gl1_shift = jnp.sum(grad_in, axis=0)
    dx = (grad_res + norm_back(grad_in, unit_in, inv_in, ln1_gain)).reshape(rows, seq, width)

    def bias_sums(d, gbup):
        sums = jnp.sum(d.astype(F32), axis=0)
        return [sums[:heads], sums[2 * heads :]] + [g[0] for g in gbup]

    shared = [gl1_gain, gl1_shift, gl2_gain, gl2_shift, jnp.sum(grad_res, axis=0), jnp.sum(up32, axis=0)]
    mine = jnp.concatenate(shared + bias_sums(d_own, [gbup_own]))
    sent = jnp.concatenate(shared + bias_sums(d_oth, [gbup0, gbup1]))
    out = (residual + y + b_down).astype(BF16).reshape(rows, seq, width)
    mine, sent, a_got, out, dx = meet([f0, f1], mine, sent, a_got, out, dx)
    att = Chain(add_low(a_own, a_got), moves)
    vec_moves = [lambda v: v + swap(v, "core")]
    vec_moves += [lambda v, s=s: v + lax.ppermute(v, s[0], s[2]) for s in steps]
    out_got = swap(out[:, half:], "mp")
    dx_got = swap(dx[:, half:].astype(BF16), "mp")
    vec = Chain(mine + swap(sent, "mp"), vec_moves)
    chains = [att, f1, f0]
    for c in chains:
        c.go()
    while att.moves:
        meet([c for c in chains if c.moves] + [vec])
        for c in chains + [vec]:
            c.go()

    block_out = join(side, out[:, :half], out_got)
    input_grad = join(side, dx[:, :half], dx_got.astype(F32))
    common = [vec.value[i * width : (i + 1) * width] for i in range(6)]
    split = vec.value[6 * width :]
    up_sum = [by_core(*c.value).astype(F32) for c in (f0, f1)]
    down_sum = [by_core(*c.value[::-1]).astype(F32) for c in (f0, f1)]
    qk_sum = by_core(*att.value).astype(F32)
    vo_sum = by_core(*att.value[::-1]).astype(F32)
    return (
        block_out,
        input_grad,
        common[0],
        common[1],
        qk_sum[:, :heads],
        split[:heads],
        qk_sum[:, heads:],
        vo_sum[:, :heads],
        split[heads : 2 * heads],
        vo_sum[:, heads:].T,
        common[4],
        common[2],
        common[3],
        jnp.concatenate(up_sum, axis=1),
        split[2 * heads :],
        jnp.concatenate(down_sum, axis=0),
        common[5],
    )


def solution(mesh):
    n_dp, n_mp = mesh.shape["dp"], mesh.shape["mp"]
    names = ("rest", "nbr", "core", "mp")
    inner = Mesh(mesh.devices.reshape(n_dp // 4, 2, 2, n_mp), names)
    dp = ("rest", "nbr", "core")
    in_specs = (
        P(dp, "mp", None),
        P(dp),
        P(dp, "mp", None),
        P(),
        P(),
        P(None, "mp"),
        P("mp"),
        P(None, "mp"),
        P(None, "mp"),
        P("mp"),
        P("mp", None),
        P(),
        P(),
        P(),
        P(None, "mp"),
        P("mp"),
        P("mp", None),
        P(),
    )
    out_specs = (
        P(dp, "mp", None),
        P(dp, "mp", None),
        P(),
        P(),
        P(None, "mp"),
        P("mp"),
        P(None, "mp"),
        P(None, "mp"),
        P("mp"),
        P("mp", None),
        P(),
        P(),
        P(),
        P(None, "mp"),
        P("mp"),
        P("mp", None),
        P(),
    )
    return jax.shard_map(
        functools.partial(on_device, dict(inner.shape)),
        mesh=inner,
        in_specs=in_specs,
        out_specs=out_specs,
        check_vma=False,
    )
```

time: 554 us -> 372 us (0.67)
  waiting for transfers between devices: 300 us -> 83.9 us
  starting transfers between devices: 22.6 us -> 52.2 us
  between operations: 15.2 us -> 2.22 us
  Pallas kernels: 90.3 us -> 103 us
  other arithmetic: 58.3 us -> 65.6 us
    psum x2 -> x0, waiting for transfers between devices: 133 us -> none  [the longest x1 73 us: on_device(): up_sum, down_sum = lax.psum((up_piece, down_piece), ('rest', 'nbr'))]
    ppermute x32 -> x26, waiting for transfers between devices: 160 us -> 41.8 us  [swap(): return lax.ppermute(value, axis, [(0, 1), (1, 0)])]
    ppermute x2 -> x21, waiting for transfers between devices: 6.94 us -> 42.2 us  [the longest x9 21.8 us: double(): return join(index, value, lax.ppermute(value, axis, perm))]
    ppermute x2 -> x21, starting transfers between devices: 2.07 us -> 32.5 us  [the longest x9 14 us: double(): return join(index, value, lax.ppermute(value, axis, perm))]
    dynamic_slice x15 -> x12, local copies, waits for them, and re-layouts: 19.3 us -> 5.47 us  [part(): return lax.dynamic_slice_in_dim(value, index * size, size, 0)]
    convert_element_type x13 -> x19, other arithmetic: 27.9 us -> 14.3 us  [the longest x17 12.8 us: add_low(): return (a.astype(F32) + b.astype(F32)).astype(BF16)]
    pallas_call x2 -> x3, Pallas kernels: 45.7 us -> 58.2 us  [ffn(): pl.pallas_call(functools.partial(ffn_kernel, (first, own), block), out_sh...]
    select_n x0 -> x9, other arithmetic: none -> 11.8 us  [the longest x7 7.84 us: by_core(): return jnp.where(core == 0, first, second)]
  transfers between devices with their start and end apart: 36 -> 47, of which waited for: 11 -> 27; matrix products, arithmetic and copies ran while one was open for 20% -> 23% of each run, Pallas kernels for 16% -> 24%
where the time goes in v2:
time: 372 us; the launch traced here: 365 us
  Pallas kernels  103 us (28%)
  waiting for transfers between devices  83.9 us (23%)
  other arithmetic  65.6 us (18%)
  starting transfers between devices  52.2 us (14%)
  local copies, waits for them, and re-layouts  35.9 us (10%)
  matrix products  22 us (6%)
    pallas_call x3, Pallas kernels, ffn(): pl.pallas_call(functools.partial(ffn_kernel, (first, own), block), out_sh...  58.2 us
    ppermute x26, waiting for transfers between devices, swap(): return lax.ppermute(value, axis, [(0, 1), (1, 0)])  41.8 us
    pallas_call x2, Pallas kernels, attend_back(): pl.pallas_call(attend_back_kernel, out_shape=jax.ShapeDtypeStruct((rows,...  26 us
    dot_general x12, matrix products, mm(): return lax.dot_general(a, b, dims, preferred_element_type=F32)  22 us
    ppermute x9, waiting for transfers between devices, double(): return join(index, value, lax.ppermute(value, axis, perm))  21.8 us
    unnamed x161, local copies, waits for them, and re-layouts  20.7 us
    ppermute x26, starting transfers between devices, swap(): return lax.ppermute(value, axis, [(0, 1), (1, 0)])  19.7 us
    pallas_call x2, Pallas kernels, attend(): pl.pallas_call(attend_kernel, out_shape=(jax.ShapeDtypeStruct((rows, seq,...  19.2 us
  transfers between devices with their start and end apart: 47, of which 27 were waited for; matrix products, arithmetic and copies ran while one was open for 23% of the time, Pallas kernels for 24%

profile of v2, /device:TPU:0, one launch (start us, length us, event | category | flops | bytes accessed | tf_op | source)
XLA Modules:
  0.0 365.3 jit_solution(16706526096928864461)
XLA Ops:
  10.1 3.0 collective-permute-start.1
  15.0 3.8 %slice_select_fusion = (bf16[768,768]{1,0:T(8,128)(2,1)}, bf16[768,768]{1,0:T(8,128)(2,1)S(1)}, bf16[768,768]{1,0:T(8,128)(2,1)S(1)}) fusion(bf16[1536,768]{1,0:T(8,128)(2,1)} %refs_4_.1, bf16[768,1536]{1,0:T(8,128)(2,1)} %refs_3_.1, pred[]{:T(512)S(6)} %eq.16), kind=kLoop, calls=%fused_computation.75 | loop fusion | flops 589824 | bytes 8257537 | tf_op jit(solution)/shard_map/jit(_where)/select_n | solution.py:361
  22.1 5.5 %collective-permute-done.1 = bf16[768,384]{0,1:T(8,128)(2,1)} collective-permute-done((bf16[768,384]{0,1:T(8,128)(2,1)}, bf16[768,384]{0,1:T(8,128)(2,1)}, u32[]{:S(2)}, u32[]{:S(2)}) %collective-permute-start.1) | collective-permute-done | bytes 589856 | tf_op jit(solution)/shard_map/ppermute | solution.py:270
  31.2 11.2 %collective-permute-done.4 = f32[2304]{0:T(1024)S(1)} collective-permute-done((f32[2304]{0:T(1024)S(1)}, f32[2304]{0:T(1024)S(1)}, u32[]{:S(2)}, u32[]{:S(2)}) %collective-permute-start.4) | collective-permute-done | bytes 9248 | tf_op jit(solution)/shard_map/ppermute | solution.py:270
  52.9 9.9 %attend.2 = (bf16[2,512,384]{2,1,0:T(8,128)(2,1)S(1)}, f32[2,3,2,512]{3,2,1,0:T(2,128)S(1)}) custom-call(s32[3]{0:T(128)S(1)} %pad_add_fusion.info, bf16[2,512,1152]{2,1,0:T(8,128)(2,1)S(1)} %bitcast.110, bf16[2,512,1152]{2,1,0:T(8,128)(2,1)S(1)} %bitcast.111, bf16[2,512,1152]{2,1,0:T(8,128)(2,1)S(1)} %bitcast.112), custom_call_target="tpu_custom_call" | custom-call | flops 11500000256 | bytes 1000 | tf_op jit(solution)/shard_map/attend/pallas_call | solution.py:108
  64.6 9.3 %attend.3 = (bf16[2,512,384]{2,1,0:T(8,128)(2,1)S(1)}, f32[2,3,2,512]{3,2,1,0:T(2,128)S(1)}) custom-call(s32[3]{0:T(128)S(1)} %pad_add_fusion.info, bf16[2,512,1152]{2,1,0:T(8,128)(2,1)S(1)} %bitcast.116, bf16[2,512,1152]{2,1,0:T(8,128)(2,1)S(1)} %bitcast.117, bf16[2,512,1152]{2,1,0:T(8,128)(2,1)S(1)} %bitcast.118), custom_call_target="tpu_custom_call" | custom-call | flops 11500000256 | bytes 1000 | tf_op jit(solution)/shard_map/attend/pallas_call | solution.py:108
  84.6 2.6 copy.44.refs_1_
  87.2 2.8 pad_maximum_fusion.2
  91.7 14.9 %ffn_other.2 = (f32[1024,768]{1,0:T(8,128)}, f32[1024,768]{1,0:T(8,128)}, bf16[1,768,768]{2,1,0:T(8,128)(2,1)S(1)}, bf16[1,768,768]{2,1,0:T(8,128)(2,1)S(1)}, f32[1,768]{1,0:T(1,128)S(1)}) custom-call(s32[1]{0:T(128)} %bitcast.info, bf16[1024,768]{1,0:T(8,128)(2,1)} %add_convert_fusion.4.refs_0_, bf16[768,1024]{1,0:T(8,128)(2,1)} %copy.44.refs_1_, ...), custom_call_target="tpu_custom_call" | custom-call | flops 17250000896 | bytes 1000 | tf_op jit(solution)/shard_map/ffn_other/pallas_call | solution.py:225
  107.2 3.4 collective-permute-done.11
  112.5 17.5 %ffn_other.3 = (f32[1024,768]{1,0:T(8,128)}, f32[1024,768]{1,0:T(8,128)}, bf16[1,768,768]{2,1,0:T(8,128)(2,1)S(1)}, bf16[1,768,768]{2,1,0:T(8,128)(2,1)S(1)}, f32[1,768]{1,0:T(1,128)S(1)}) custom-call(s32[1]{0:T(128)} %bitcast.info, bf16[1024,768]{1,0:T(8,128)(2,1)} %add_convert_fusion.4.refs_0_, ...), custom_call_target="tpu_custom_call", output_to_operand_aliasing={{0}: (7, {}), {1}: (8, {})} | custom-call | flops 17250000896 | bytes 1000 | tf_op jit(solution)/shard_map/ffn_other/pallas_call | solution.py:225
  131.8 25.8 %ffn_own.1 = (f32[1024,768]{1,0:T(8,128)}, f32[1024,768]{1,0:T(8,128)}, bf16[2,768,768]{2,1,0:T(8,128)(2,1)}, bf16[2,768,768]{2,1,0:T(8,128)(2,1)}, f32[1,1536]{1,0:T(1,128)S(1)}) custom-call(s32[1]{0:T(128)} %bitcast.info, bf16[1024,768]{1,0:T(8,128)(2,1)S(1)} %copy-done.1, ...), custom_call_target="tpu_custom_call", output_to_operand_aliasing={{0}: (7, {}), {1}: (8, {})} | custom-call | flops 25300000768 | bytes 1000 | tf_op jit(solution)/shard_map/ffn_own/pallas_call | solution.py:225
  160.1 4.0 %multiply_reduce_fusion = (f32[768]{0:T(1024)S(1)}, f32[1024]{0:T(1024)S(1)}, f32[1024]{0:T(1024)S(1)}, f32[768]{0:T(1024)S(1)}) fusion(f32[1024,768]{1,0:T(8,128)} %get-tuple-element.139, f32[1024,768]{1,0:T(8,128)} %copy-done.4, f32[1024]{0:T(1024)S(1)} %add_rsqrt_fusion, f32[1024]{0:T(1024)S(1)} %broadcast_multiply_fusion.4, f32[768]{0:T(1024)S(1)} %copy-done.55), kind=kLoop, calls=%fused_computation.30 | loop fusion | flops 7074304 | bytes 6317056 | tf_op jit(solution)/shard_map/reduce_sum | solution.py:443
  164.2 4.1 %fusion.29 = (f32[768]{0:T(1024)S(1)}, f32[1024,768]{1,0:T(8,128)S(1)}, bf16[1024,768]{1,0:T(8,128)(2,1)}) fusion(f32[1024]{0:T(1024)S(1)} %get-tuple-element.271, f32[1024,768]{1,0:T(8,128)S(1)} %copy-done.6, f32[1024]{0:T(1024)S(1)} %broadcast_multiply_fusion.4, f32[1024]{0:T(1024)S(1)} %get-tuple-element.272, f32[1024,768]{1,0:T(8,128)S(1)} %copy-done.13, ...), kind=kLoop, calls=%fused_computation.154 | loop fusion | flops 10222848 | bytes 15754240 | tf_op jit(solution)/shard_map/reduce_sum | solution.py:488
  179.6 12.9 %attend_back.2 = bf16[2,512,1152]{2,1,0:T(8,128)(2,1)S(1)} custom-call(s32[3]{0:T(128)S(1)} %pad_add_fusion.info, bf16[2,512,1152]{2,1,0:T(8,128)(2,1)} %bitcast.119, bf16[2,512,1152]{2,1,0:T(8,128)(2,1)} %bitcast.120, bf16[2,512,1152]{2,1,0:T(8,128)(2,1)} %bitcast.121, bf16[2,512,384]{2,1,0:T(8,128)(2,1)S(1)} %bitcast.123, ...), custom_call_target="tpu_custom_call" | custom-call | flops 14949999616 | bytes 1000 | tf_op jit(solution)/shard_map/attend_back/pallas_call | solution.py:132
  200.3 2.6 convolution_convert_fusion.4
  211.7 13.1 %attend_back.3 = bf16[2,512,1152]{2,1,0:T(8,128)(2,1)S(1)} custom-call(s32[3]{0:T(128)S(1)} %pad_add_fusion.info, bf16[2,512,1152]{2,1,0:T(8,128)(2,1)} %bitcast.113, bf16[2,512,1152]{2,1,0:T(8,128)(2,1)} %bitcast.114, bf16[2,512,1152]{2,1,0:T(8,128)(2,1)} %bitcast.115, bf16[2,512,384]{2,1,0:T(8,128)(2,1)S(1)} %bitcast.122, ...), custom_call_target="tpu_custom_call" | custom-call | flops 14949999616 | bytes 1000 | tf_op jit(solution)/shard_map/attend_back/pallas_call | solution.py:132
  232.2 2.6 collective-permute-start.20
  236.7 5.2 %collective-permute-done.20 = bf16[96,768]{1,0:T(8,128)(2,1)S(1)} collective-permute-done((bf16[96,768]{1,0:T(8,128)(2,1)S(1)}, bf16[96,768]{1,0:T(8,128)(2,1)S(1)}, u32[]{:S(2)}, u32[]{:S(2)}) %collective-permute-start.20) | collective-permute-done | bytes 147488 | tf_op jit(solution)/shard_map/ppermute | solution.py:302
  242.0 4.5 %collective-permute-done.23 = bf16[192,768]{1,0:T(8,128)(2,1)S(1)} collective-permute-done((bf16[192,768]{1,0:T(8,128)(2,1)S(1)}, bf16[192,768]{1,0:T(8,128)(2,1)S(1)}, u32[]{:S(2)}, u32[]{:S(2)}) %collective-permute-start.23) | collective-permute-done | bytes 294944 | tf_op jit(solution)/shard_map/ppermute | solution.py:302
  248.6 3.1 fusion.10
  253.5 7.2 %collective-permute-done.22 = bf16[96,768]{1,0:T(8,128)(2,1)S(1)} collective-permute-done((bf16[96,768]{1,0:T(8,128)(2,1)S(1)}, bf16[96,768]{1,0:T(8,128)(2,1)S(1)}, u32[]{:S(2)}, u32[]{:S(2)}) %collective-permute-start.22) | collective-permute-done | bytes 147488 | tf_op jit(solution)/shard_map/ppermute | solution.py:308
  269.4 2.9 collective-permute-done.30
  282.5 2.9 collective-permute-start.32
  286.6 3.3 collective-permute-done.32
  296.8 2.5 collective-permute-start.36
  303.3 2.6 collective-permute-done.36
  322.4 2.8 collective-permute-start.42
  331.6 2.8 maximum_select_fusion.1
  334.4 13.4 %collective-permute-done.26 = bf16[2,256,768]{2,1,0:T(8,128)(2,1)} collective-permute-done((bf16[2,256,768]{2,1,0:T(8,128)(2,1)}, bf16[2,256,768]{2,1,0:T(8,128)(2,1)}, u32[]{:S(2)}, u32[]{:S(2)}) %collective-permute-start.26) | collective-permute-done | bytes 786464 | tf_op jit(solution)/shard_map/ppermute | solution.py:270
  355.3 2.5 maximum_convert_fusion.1
  357.9 2.8 maximum_convert_fusion
  (355 shorter events, 155.6 us)
Async XLA Ops:
  10.1 17.5 %collective-permute-start.1 = (bf16[768,384]{0,1:T(8,128)(2,1)}, bf16[768,384]{0,1:T(8,128)(2,1)}, u32[]{:S(2)}, u32[]{:S(2)}) collective-permute-start(bf16[768,384]{0,1:T(8,128)(2,1)} %fusion.21), channel_id=1, source_target_pairs={{0,1},{1,0},{2,3},{3,2},{4,5},{5,4},{6,7},{7,6},{8,9},{9,8},{10,11... | collective-permute-start | bytes 1769480 | tf_op jit(solution)/shard_map/ppermute | solution.py:270
  13.1 29.4 %collective-permute-start = (bf16[2,256,768]{2,1,0:T(8,128)(2,1)}, bf16[2,256,768]{2,1,0:T(8,128)(2,1)S(1)}, u32[]{:S(2)}, u32[]{:S(2)}) collective-permute-start(bf16[2,256,768]{2,1,0:T(8,128)(2,1)} %get-tuple-element.102), channel_id=1, source_target_pairs={{0,1},{1,0},{2,3},{3,2},{4,5},{5,4},{6,7},{7,6},{8,9},{9,8},{10,11... | collective-permute-start | bytes 2359304 | tf_op jit(solution)/shard_map/ppermute | solution.py:270
  27.7 14.7 %collective-permute-start.4 = (f32[2304]{0:T(1024)S(1)}, f32[2304]{0:T(1024)S(1)}, u32[]{:S(2)}, u32[]{:S(2)}) collective-permute-start(f32[2304]{0:T(1024)S(1)} %pad_maximum_fusion.7), channel_id=1, source_target_pairs={{0,1},{1,0},{2,3},{3,2},{4,5},{5,4},{6,7},{7,6},{8,9},{9,8},{10,11... | collective-permute-start | bytes 27656 | tf_op jit(solution)/shard_map/ppermute | solution.py:270
  29.7 13.1 %collective-permute-start.2 = (bf16[768,384]{0,1:T(8,128)(2,1)}, bf16[768,384]{0,1:T(8,128)(2,1)S(1)}, u32[]{:S(2)}, u32[]{:S(2)}) collective-permute-start(bf16[768,384]{0,1:T(8,128)(2,1)} %collective-permute-done.1), channel_id=1, source_target_pairs={{0,4},{4,0},{1,5},{5,1},{2,6},{6,2},{3,7},{7,3},{8,12},{12,8},{9,1... | collective-permute-start | bytes 1769480 | tf_op jit(solution)/shard_map/ppermute | solution.py:270
  45.1 17.7 %collective-permute-start.5 = (bf16[384,768]{1,0:T(8,128)(2,1)S(1)}, bf16[384,768]{1,0:T(8,128)(2,1)}, u32[]{:S(2)}, u32[]{:S(2)}) collective-permute-start(bf16[384,768]{1,0:T(8,128)(2,1)S(1)} %dynamic-slice_select_fusion), channel_id=1, source_target_pairs={{0,1},{1,0},{2,3},{3,2},{4,5},{5,4},{6,7},{7,6},{8,9},{9,8},{10,11... | collective-permute-start | bytes 1769480 | tf_op jit(solution)/shard_map/ppermute | solution.py:270
  46.9 33.0 %collective-permute-start.7 = (bf16[2,256,768]{2,1,0:T(8,128)(2,1)}, bf16[2,256,768]{2,1,0:T(8,128)(2,1)S(1)}, u32[]{:S(2)}, u32[]{:S(2)}) collective-permute-start(bf16[2,256,768]{2,1,0:T(8,128)(2,1)} %get-tuple-element.115), channel_id=1, source_target_pairs={{0,1},{1,0},{2,3},{3,2},{4,5},{5,4},{6,7},{7,6},{8,9},{9,8},{10,11... | collective-permute-start | bytes 2359304 | tf_op jit(solution)/shard_map/ppermute | solution.py:270
  62.8 15.5 %collective-permute-start.6 = (bf16[384,768]{1,0:T(8,128)(2,1)}, bf16[384,768]{1,0:T(8,128)(2,1)S(1)}, u32[]{:S(2)}, u32[]{:S(2)}) collective-permute-start(bf16[384,768]{1,0:T(8,128)(2,1)} %collective-permute-done.5), channel_id=1, source_target_pairs={{0,4},{4,0},{1,5},{5,1},{2,6},{6,2},{3,7},{7,3},{8,12},{12,8},{9,1... | collective-permute-start | bytes 1769480 | tf_op jit(solution)/shard_map/ppermute | solution.py:270
  73.9 32.7 %collective-permute-start.9 = (bf16[768,768]{1,0:T(8,128)(2,1)}, bf16[768,768]{1,0:T(8,128)(2,1)}, u32[]{:S(2)}, u32[]{:S(2)}) collective-permute-start(bf16[768,768]{1,0:T(8,128)(2,1)} %get-tuple-element.121), channel_id=1, source_target_pairs={{0,1},{1,0},{2,3},{3,2},{4,5},{5,4},{6,7},{7,6},{8,9},{9,8},{10,11... | collective-permute-start | bytes 3538952 | tf_op jit(solution)/shard_map/ppermute | solution.py:270
  79.9 11.8 %collective-permute-start.8 = (bf16[768,768]{1,0:T(8,128)(2,1)S(1)}, bf16[768,768]{1,0:T(8,128)(2,1)}, u32[]{:S(2)}, u32[]{:S(2)}) collective-permute-start(bf16[768,768]{1,0:T(8,128)(2,1)S(1)} %maximum_select_fusion.3.refs_3_), channel_id=1, source_target_pairs={{0,2},{2,0},{1,3},{3,1},{4,6},{6,4},{5,7},{7,5},{8,10},{10,8},{9,1... | collective-permute-start | bytes 3538952 | tf_op jit(solution)/shard_map/ppermute | solution.py:270
  130.0 28.9 %collective-permute-start.12 = (bf16[768,768]{1,0:T(8,128)(2,1)S(1)}, bf16[768,768]{1,0:T(8,128)(2,1)}, u32[]{:S(2)}, u32[]{:S(2)}) collective-permute-start(bf16[768,768]{1,0:T(8,128)(2,1)S(1)} %fusion.19), channel_id=1, source_target_pairs={{0,1},{1,0},{2,3},{3,2},{4,5},{5,4},{6,7},{7,6},{8,9},{9,8},{10,11... | collective-permute-start | bytes 3538952 | tf_op jit(solution)/shard_map/ppermute | solution.py:270
  131.7 25.9 %collective-permute-start.13 = (bf16[768,768]{1,0:T(8,128)(2,1)S(1)}, bf16[768,768]{1,0:T(8,128)(2,1)S(1)}, u32[]{:S(2)}, u32[]{:S(2)}) collective-permute-start(bf16[768,768]{1,0:T(8,128)(2,1)S(1)} %bitcast.108), channel_id=1, source_target_pairs={{0,2},{2,0},{1,3},{3,1},{4,6},{6,4},{5,7},{7,5},{8,10},{10,8},{9,1... | collective-permute-start | bytes 3538952 | tf_op jit(solution)/shard_map/ppermute | solution.py:270
  158.9 13.7 %collective-permute-start.14 = (bf16[2,768,768]{2,1,0:T(8,128)(2,1)}, bf16[2,768,768]{2,1,0:T(8,128)(2,1)}, u32[]{:S(2)}, u32[]{:S(2)}) collective-permute-start(bf16[2,768,768]{2,1,0:T(8,128)(2,1)} %get-tuple-element.137), channel_id=1, source_target_pairs={{0,2},{2,0},{1,3},{3,1},{4,6},{6,4},{5,7},{7,5},{8,10},{10,8},{9,1... | collective-permute-start | bytes 7077896 | tf_op jit(solution)/shard_map/ppermute | solution.py:270
  159.3 35.1 %collective-permute-start.16 = (bf16[768,768]{1,0:T(8,128)(2,1)}, bf16[768,768]{1,0:T(8,128)(2,1)S(1)}, u32[]{:S(2)}, u32[]{:S(2)}) collective-permute-start(bf16[768,768]{1,0:T(8,128)(2,1)} %fusion.18), channel_id=1, source_target_pairs={{0,1},{1,0},{2,3},{3,2},{4,5},{5,4},{6,7},{7,6},{8,9},{9,8},{10,11... | collective-permute-start | bytes 3538952 | tf_op jit(solution)/shard_map/ppermute | solution.py:270
  178.0 15.5 %collective-permute-start.15 = (bf16[384,768]{1,0:T(8,128)(2,1)S(1)}, bf16[384,768]{1,0:T(8,128)(2,1)S(1)}, u32[]{:S(2)}, u32[]{:S(2)}) collective-permute-start(bf16[384,768]{1,0:T(8,128)(2,1)S(1)} %constant_dynamic-slice_fusion.8), channel_id=1, source_target_pairs={{0,4},{4,0},{1,5},{5,1},{2,6},{6,2},{3,7},{7,3},{8,12},{12,8},{9,1... | collective-permute-start | bytes 1769480 | tf_op jit(solution)/shard_map/ppermute | solution.py:302
  208.4 16.4 %collective-permute-start.18 = (bf16[192,768]{1,0:T(8,128)(2,1)S(1)}, bf16[192,768]{1,0:T(8,128)(2,1)S(1)}, u32[]{:S(2)}, u32[]{:S(2)}) collective-permute-start(bf16[192,768]{1,0:T(8,128)(2,1)S(1)} %constant_dynamic-slice_fusion.7), channel_id=1, source_target_pairs={{0,8},{8,0},{16,24},{24,16},{1,9},{9,1},{17,25},{25,17},{2,10},{10... | collective-permute-start | bytes 884744 | tf_op jit(solution)/shard_map/ppermute | solution.py:302
  210.1 15.5 %collective-permute-start.19 = (bf16[384,768]{1,0:T(8,128)(2,1)S(1)}, bf16[384,768]{1,0:T(8,128)(2,1)S(1)}, u32[]{:S(2)}, u32[]{:S(2)}) collective-permute-start(bf16[384,768]{1,0:T(8,128)(2,1)S(1)} %constant_dynamic-slice_fusion.6), channel_id=1, source_target_pairs={{0,4},{4,0},{1,5},{5,1},{2,6},{6,2},{3,7},{7,3},{8,12},{12,8},{9,1... | collective-permute-start | bytes 1769480 | tf_op jit(solution)/shard_map/ppermute | solution.py:302
  228.8 17.8 %collective-permute-start.21 = (bf16[768,768]{1,0:T(8,128)(2,1)S(1)}, bf16[768,768]{1,0:T(8,128)(2,1)S(1)}, u32[]{:S(2)}, u32[]{:S(2)}) collective-permute-start(bf16[768,768]{1,0:T(8,128)(2,1)S(1)} %broadcast_select_fusion.5), channel_id=1, source_target_pairs={{0,2},{2,0},{1,3},{3,1},{4,6},{6,4},{5,7},{7,5},{8,10},{10,8},{9,1... | collective-permute-start | bytes 3538952 | tf_op jit(solution)/shard_map/ppermute | solution.py:270
  232.2 9.8 %collective-permute-start.20 = (bf16[96,768]{1,0:T(8,128)(2,1)S(1)}, bf16[96,768]{1,0:T(8,128)(2,1)S(1)}, u32[]{:S(2)}, u32[]{:S(2)}) collective-permute-start(bf16[96,768]{1,0:T(8,128)(2,1)S(1)} %constant_dynamic-slice_fusion.5), channel_id=1, source_target_pairs={{0,16},{8,24},{16,0},{24,8},{1,17},{9,25},{17,1},{25,9},{2,18},{10... | collective-permute-start | bytes 442376 | tf_op jit(solution)/shard_map/ppermute | solution.py:302
  234.8 11.7 %collective-permute-start.23 = (bf16[192,768]{1,0:T(8,128)(2,1)S(1)}, bf16[192,768]{1,0:T(8,128)(2,1)S(1)}, u32[]{:S(2)}, u32[]{:S(2)}) collective-permute-start(bf16[192,768]{1,0:T(8,128)(2,1)S(1)} %constant_dynamic-slice_fusion.4), channel_id=1, source_target_pairs={{0,8},{8,0},{16,24},{24,16},{1,9},{9,1},{17,25},{25,17},{2,10},{10... | collective-permute-start | bytes 884744 | tf_op jit(solution)/shard_map/ppermute | solution.py:302
  235.7 27.3 %collective-permute-start.24 = (bf16[768,768]{1,0:T(8,128)(2,1)S(1)}, bf16[768,768]{1,0:T(8,128)(2,1)S(1)}, u32[]{:S(2)}, u32[]{:S(2)}) collective-permute-start(bf16[768,768]{1,0:T(8,128)(2,1)S(1)} %add_convert_fusion.7), channel_id=1, source_target_pairs={{0,1},{1,0},{2,3},{3,2},{4,5},{5,4},{6,7},{7,6},{8,9},{9,8},{10,11... | collective-permute-start | bytes 3538952 | tf_op jit(solution)/shard_map/ppermute | solution.py:270
  265.2 14.0 %collective-permute-start.27 = (bf16[384,768]{1,0:T(8,128)(2,1)}, bf16[384,768]{1,0:T(8,128)(2,1)}, u32[]{:S(2)}, u32[]{:S(2)}) collective-permute-start(bf16[384,768]{1,0:T(8,128)(2,1)} %constant_dynamic-slice_fusion.3), channel_id=1, source_target_pairs={{0,4},{4,0},{1,5},{5,1},{2,6},{6,2},{3,7},{7,3},{8,12},{12,8},{9,1... | collective-permute-start | bytes 1769480 | tf_op jit(solution)/shard_map/ppermute | solution.py:302
  266.9 9.9 %collective-permute-start.29 = (bf16[192,768]{1,0:T(8,128)(2,1)}, bf16[192,768]{1,0:T(8,128)(2,1)}, u32[]{:S(2)}, u32[]{:S(2)}) collective-permute-start(bf16[192,768]{1,0:T(8,128)(2,1)} %maximum_select_fusion.10), channel_id=1, source_target_pairs={{0,8},{8,0},{16,24},{24,16},{1,9},{9,1},{17,25},{25,17},{2,10},{10... | collective-permute-start | bytes 884744 | tf_op jit(solution)/shard_map/ppermute | solution.py:308
  280.4 12.8 %collective-permute-start.33 = (bf16[384,768]{1,0:T(8,128)(2,1)S(1)}, bf16[384,768]{1,0:T(8,128)(2,1)S(1)}, u32[]{:S(2)}, u32[]{:S(2)}) collective-permute-start(bf16[384,768]{1,0:T(8,128)(2,1)S(1)} %maximum_select_fusion.7), channel_id=1, source_target_pairs={{0,4},{4,0},{1,5},{5,1},{2,6},{6,2},{3,7},{7,3},{8,12},{12,8},{9,1... | collective-permute-start | bytes 1769480 | tf_op jit(solution)/shard_map/ppermute | solution.py:308
  281.3 9.9 %collective-permute-start.31 = (bf16[192,768]{1,0:T(8,128)(2,1)S(1)}, bf16[192,768]{1,0:T(8,128)(2,1)S(1)}, u32[]{:S(2)}, u32[]{:S(2)}) collective-permute-start(bf16[192,768]{1,0:T(8,128)(2,1)S(1)} %constant_dynamic-slice_fusion.1), channel_id=1, source_target_pairs={{0,8},{8,0},{16,24},{24,16},{1,9},{9,1},{17,25},{25,17},{2,10},{10... | collective-permute-start | bytes 884744 | tf_op jit(solution)/shard_map/ppermute | solution.py:302
  296.8 9.0 %collective-permute-start.36 = (bf16[192,768]{1,0:T(8,128)(2,1)S(1)}, bf16[192,768]{1,0:T(8,128)(2,1)S(1)}, u32[]{:S(2)}, u32[]{:S(2)}) collective-permute-start(bf16[192,768]{1,0:T(8,128)(2,1)S(1)} %maximum_select_fusion.11), channel_id=1, source_target_pairs={{0,8},{8,0},{16,24},{24,16},{1,9},{9,1},{17,25},{25,17},{2,10},{10... | collective-permute-start | bytes 884744 | tf_op jit(solution)/shard_map/ppermute | solution.py:308
  306.0 13.8 %collective-permute-start.39 = (bf16[384,768]{1,0:T(8,128)(2,1)S(1)}, bf16[384,768]{1,0:T(8,128)(2,1)S(1)}, u32[]{:S(2)}, u32[]{:S(2)}) collective-permute-start(bf16[384,768]{1,0:T(8,128)(2,1)S(1)} %maximum_select_fusion.8), channel_id=1, source_target_pairs={{0,4},{4,0},{1,5},{5,1},{2,6},{6,2},{3,7},{7,3},{8,12},{12,8},{9,1... | collective-permute-start | bytes 1769480 | tf_op jit(solution)/shard_map/ppermute | solution.py:308
  307.8 43.2 %collective-permute-start.45 = (bf16[768,768]{1,0:T(8,128)(2,1)}, bf16[768,768]{1,0:T(8,128)(2,1)}, u32[]{:S(2)}, u32[]{:S(2)}) collective-permute-start(bf16[768,768]{1,0:T(8,128)(2,1)} %maximum_select_fusion.4), channel_id=1, source_target_pairs={{0,2},{2,0},{1,3},{3,1},{4,6},{6,4},{5,7},{7,5},{8,10},{10,8},{9,1... | collective-permute-start | bytes 3538952 | tf_op jit(solution)/shard_map/ppermute | solution.py:270
  307.8 10.3 %collective-permute-start.38 = (bf16[96,768]{1,0:T(8,128)(2,1)S(1)}, bf16[96,768]{1,0:T(8,128)(2,1)S(1)}, u32[]{:S(2)}, u32[]{:S(2)}) collective-permute-start(bf16[96,768]{1,0:T(8,128)(2,1)S(1)} %add_convert_fusion.14), channel_id=1, source_target_pairs={{0,16},{8,24},{16,0},{24,8},{1,17},{9,25},{17,1},{25,9},{2,18},{10... | collective-permute-start | bytes 442376 | tf_op jit(solution)/shard_map/ppermute | solution.py:308
  310.9 20.7 %collective-permute-start.25 = (bf16[2,256,768]{2,1,0:T(8,128)(2,1)}, bf16[2,256,768]{2,1,0:T(8,128)(2,1)}, u32[]{:S(2)}, u32[]{:S(2)}) collective-permute-start(bf16[2,256,768]{2,1,0:T(8,128)(2,1)} %get-tuple-element.232), channel_id=1, source_target_pairs={{0,1},{1,0},{2,3},{3,2},{4,5},{5,4},{6,7},{7,6},{8,9},{9,8},{10,11... | collective-permute-start | bytes 2359304 | tf_op jit(solution)/shard_map/ppermute | solution.py:270
  315.8 32.0 %collective-permute-start.26 = (bf16[2,256,768]{2,1,0:T(8,128)(2,1)}, bf16[2,256,768]{2,1,0:T(8,128)(2,1)}, u32[]{:S(2)}, u32[]{:S(2)}) collective-permute-start(bf16[2,256,768]{2,1,0:T(8,128)(2,1)} %slice.223), channel_id=1, source_target_pairs={{0,1},{1,0},{2,3},{3,2},{4,5},{5,4},{6,7},{7,6},{8,9},{9,8},{10,11... | collective-permute-start | bytes 2359304 | tf_op jit(solution)/shard_map/ppermute | solution.py:270
  327.4 27.7 %collective-permute-start.46 = (bf16[768,768]{1,0:T(8,128)(2,1)S(1)}, bf16[768,768]{1,0:T(8,128)(2,1)S(1)}, u32[]{:S(2)}, u32[]{:S(2)}) collective-permute-start(bf16[768,768]{1,0:T(8,128)(2,1)S(1)} %copy-done.21), channel_id=1, source_target_pairs={{0,2},{2,0},{1,3},{3,1},{4,6},{6,4},{5,7},{7,5},{8,10},{10,8},{9,1... | collective-permute-start | bytes 3538952 | tf_op jit(solution)/shard_map/ppermute | solution.py:270
  330.3 22.5 %collective-permute-start.43 = (bf16[384,768]{1,0:T(8,128)(2,1)S(1)}, bf16[384,768]{1,0:T(8,128)(2,1)S(1)}, u32[]{:S(2)}, u32[]{:S(2)}) collective-permute-start(bf16[384,768]{1,0:T(8,128)(2,1)S(1)} %maximum_select_fusion.9), channel_id=1, source_target_pairs={{0,4},{4,0},{1,5},{5,1},{2,6},{6,2},{3,7},{7,3},{8,12},{12,8},{9,1... | collective-permute-start | bytes 1769480 | tf_op jit(solution)/shard_map/ppermute | solution.py:308
  (86 other events, 446.2 us)
